TPU v7x, 256 devices: a whole 4x4x8 slice. The times are simulated.
256 devices in a mesh: sib: 2 (over core), row: 8 (over z), col: 16 (over x, y).
Axes of the slice: x: 4, y: 4, z: 8, core: 2. Of those that a mesh axis runs over, the one named last changes fastest.
Arguments:
- front_inverse: bfloat16 [24576, 24576], P('row', 'col'), may hold values from -0.078125 to 0.078125
- panel: bfloat16 [2, 12288, 256], P('sib', 'col'), may hold values from -0.59765625 to 0.59765625
- row_map: int32 [2, 12288], P('sib'), may hold values from 0 to 24575, as said below
- diag_inverse: float32 [2, 256, 256], P('sib'), may hold values from -6 to 6
Outputs:
- offdiag_block: float32 [2, 24576, 256], P('sib', ('row', 'col'))
- diag_block: float32 [2, 256, 256], P('sib')
Inputs may be any that keep to these rules, and one draw needn't show every extreme that they name: Each row of row_map names 12288 different front rows in increasing order, the first 0 and the last 24575.
All inputs are finite; a program needn't handle non-finite values.
Results may differ from a plain program's by a relative error of at most 0.0003.
Values may be sent and summed in bfloat16 or wider, within the bound.
A program may use at most 64 MiB of HBM per device.

v0:
```python
import math

import jax
import jax.numpy as jnp
from jax import lax
from jax.sharding import Mesh
from jax.sharding import PartitionSpec as P

COL = ("col_0", "col_1")
ROW_COL = ("row", "col_0", "col_1")


def rows_for(lines, count):
    spare = -len(lines) % count
    return jnp.pad(lines, [(0, spare)] + [(0, 0)] * (lines.ndim - 1))


def copy_for_each(x, axis):
    count = lax.axis_size(axis)
    return lax.all_to_all(jnp.broadcast_to(x[None], (count, *x.shape)), axis, 0, 0, tiled=True)


def in_order(tiles, dim):
    tiles = jnp.moveaxis(tiles, 0, dim)
    lengths = tiles.shape
    return tiles.reshape(*lengths[:dim], lengths[dim] * lengths[dim + 1], *lengths[dim + 2 :])


def gather_axes(x, axes, dim):
    far, near = axes
    first = copy_for_each(x, far)
    tiles = jnp.swapaxes(copy_for_each(first, near), 0, 1)
    return in_order(tiles.reshape(-1, *x.shape), dim)


def cut_along(x, dim, count):
    lengths = x.shape
    tiles = x.reshape(*lengths[:dim], count, lengths[dim] // count, *lengths[dim + 1 :])
    return jnp.moveaxis(tiles, dim, 0)


def sum_at_owner(x, axis, dim):
    count = lax.axis_size(axis)
    tiles = lax.all_to_all(cut_along(x, dim, count), axis, 0, 0, tiled=True)
    return jnp.sum(tiles, axis=0)


def sum_in_two_steps(x, axes, dim):
    far, near = axes
    tiles = cut_along(x, dim, lax.axis_size(far))
    nearer = sum_at_owner(tiles, near, dim + 1)
    arrived = lax.all_to_all(nearer, far, split_axis=0, concat_axis=0, tiled=True)
    return arrived.sum(axis=0)


def total_of(x, axes):
    lines = x.reshape(-1, x.shape[-1])
    padded = rows_for(lines, lax.axis_size(axes[0]) * lax.axis_size(axes[1]))
    whole = gather_axes(sum_in_two_steps(padded, axes, 0), axes, 0)
    return lax.slice_in_dim(whole, 0, len(lines)).reshape(x.shape)


def spread_range(padded_rows, padded_places, places, lower, count):
    blk = math.gcd(count, 128)
    nblk = count // blk
    starts = lower + jnp.arange(nblk, dtype=jnp.int32) * blk
    first = jnp.searchsorted(places, starts)

    def window(begin):
        rows = lax.dynamic_slice_in_dim(padded_rows, begin, blk, 0)
        marks = lax.dynamic_slice_in_dim(padded_places, begin, blk, 0)
        return (rows, marks)

    rows, marks = jax.vmap(window)(first)
    target = starts[:, None] + jnp.arange(blk, dtype=jnp.int32)[None, :]
    onehot = marks[:, None, :] == target[:, :, None]
    table = onehot.astype(jnp.bfloat16)
    spread = jnp.einsum("njk,nkw->njw", table, rows, preferred_element_type=jnp.float32)
    hits = jnp.sum(onehot.astype(jnp.float32), axis=2)
    return (spread.astype(jnp.bfloat16).reshape(count, rows.shape[2]), hits.reshape(count))


def shards(front_inverse, panel, row_map, diag_inverse):
    row_index = lax.axis_index("row")
    col_index = lax.axis_index(COL)
    ncol = lax.axis_size(COL)
    front_rows, front_cols = front_inverse.shape
    share = front_rows // ncol
    width = panel.shape[2]
    col_lower = col_index * front_cols
    row_lower = row_index * front_rows
    places_all = row_map[0]
    whole_panel = lax.all_gather(panel, COL, axis=1, tiled=True)[0]
    padded_rows = jnp.concatenate([whole_panel, jnp.zeros((128, width), jnp.bfloat16)], axis=0)
    total_front = front_rows * lax.axis_size("row")
    padded_places = jnp.concatenate([places_all, jnp.full((128,), total_front, jnp.int32)], axis=0)
    spread_cols, unused_hits = spread_range(
        padded_rows, padded_places, places_all, col_lower, front_cols
    )
    spread_rows, row_hits = spread_range(
        padded_rows, padded_places, places_all, row_lower, front_rows
    )
    share_hits = lax.dynamic_slice_in_dim(row_hits, col_index * share, share, 0)
    partial_value = jnp.dot(front_inverse, spread_cols, preferred_element_type=jnp.float32)
    local_terms = jnp.dot(
        spread_rows.astype(jnp.float32).T, partial_value, precision=lax.Precision.HIGHEST
    )
    diag_terms = total_of(local_terms, (("row", "col_0"), "col_1"))
    product = sum_at_owner(partial_value, COL, 0)
    offdiag = jnp.where(share_hits[:, None] > 0.5, -product, jnp.zeros_like(product))
    diag = diag_inverse[0] + diag_terms
    return (offdiag[None], diag[None])


def solution(mesh):
    finer = Mesh(
        mesh.devices.reshape(mesh.shape["sib"], mesh.shape["row"], 4, 4),
        ("sib", "row", "col_0", "col_1"),
    )
    return jax.shard_map(
        shards,
        mesh=finer,
        in_specs=(P("row", COL), P("sib", COL, None), P("sib", None), P("sib", None, None)),
        out_specs=(P("sib", ROW_COL, None), P("sib", None, None)),
        check_vma=False,
    )
```

profile of v0, /device:TPU:20, one launch (start us, length us, event | category | flops | bytes accessed | tf_op | source)
XLA Modules:
  0.0 309.4 jit_solution(812381985895339605)
XLA Ops:
  8.0 21.8 %while.56 = (s32[]{:T(128)}, u32[24]{0:T(128)S(1)}, u32[24]{0:T(128)S(1)}, s32[12288]{0:T(1024)}, s32[]{:T(128)}, /*index=5*/s32[]{:T(128)}, s32[]{:T(128)}, s32[]{}) while((s32[]{:T(128)}, u32[24]{0:T(128)S(1)}, u32[24]{0:T(128)S(1)}, s32[12288]{0:T(1024)}, s32[]{:T(128)}, /*index=5*/s32[]{:T(128)}, s32[]{:T(128)}, s32[]{}) %tuple.129), condition=%wide.region_1.2_spmd.clone, body=%wide.region_0.1_spmd.clone.sunk | while | flops 1388 | bytes 5360 | solution.py:67
  8.0 1.5 gather_fusion
  9.6 1.5 gather_fusion
  11.1 1.5 gather_fusion
  12.7 1.5 gather_fusion
  15.8 1.5 gather_fusion
  17.4 1.5 gather_fusion
  20.5 1.5 gather_fusion
  23.6 1.5 gather_fusion
  25.2 1.5 gather_fusion
  26.7 1.5 gather_fusion
  29.9 21.3 %while.57 = (s32[]{:T(128)}, u32[12]{0:T(128)S(1)}, u32[12]{0:T(128)S(1)}, s32[12288]{0:T(1024)}, s32[]{:T(128)}, /*index=5*/s32[]{:T(128)}, s32[]{:T(128)}, s32[]{}) while((s32[]{:T(128)}, u32[12]{0:T(128)S(1)}, u32[12]{0:T(128)S(1)}, s32[12288]{0:T(1024)}, s32[]{:T(128)}, /*index=5*/s32[]{:T(128)}, s32[]{:T(128)}, s32[]{}) %tuple.130), condition=%wide.region_4.5_spmd.clone, body=%wide.region_3.4_spmd.clone.sunk | while | flops 1208 | bytes 4784 | solution.py:67
  52.1 16.0 %while.53 = (s32[]{:T(128)}, s32[12416]{0:T(1024)S(1)}, s32[12,1]{0,1:T(1,128)S(1)}, s32[12,128]{1,0:T(8,128)S(1)}, s32[]{:T(128)}, /*index=5*/s32[]{:T(128)}) while((s32[]{:T(128)}, s32[12416]{0:T(1024)S(1)}, s32[12,1]{0,1:T(1,128)S(1)}, s32[12,128]{1,0:T(8,128)S(1)}, s32[]{:T(128)}, /*index=5*/s32[]{:T(128)}) %tuple.115), condition=%wide.while_cond.1, body=%wide.while_body.1.sunk | while | flops 2 | bytes 2145 | solution.py:71
  68.2 32.0 %while.52 = (s32[]{:T(128)}, s32[12416]{0:T(1024)S(1)}, s32[24,1]{0,1:T(1,128)S(1)}, s32[24,128]{1,0:T(8,128)S(1)}, s32[]{:T(128)}, /*index=5*/s32[]{:T(128)}) while((s32[]{:T(128)}, s32[12416]{0:T(1024)S(1)}, s32[24,1]{0,1:T(1,128)S(1)}, s32[24,128]{1,0:T(8,128)S(1)}, s32[]{:T(128)}, /*index=5*/s32[]{:T(128)}) %tuple.132), condition=%wide.while_cond, body=%wide.while_body.sunk | while | flops 2 | bytes 2145 | solution.py:71
  100.2 6.4 %concatenate.13 = bf16[12416,256]{1,0:T(8,128)(2,1)} pad(bf16[12288,256]{1,0:T(8,128)(2,1)} %bitcast.58, bf16[]{:T(256)} %constant.99.clone.1), padding=0_128x0_0 | pad | bytes 12648450 | tf_op jit(solution)/shard_map/concatenate | solution.py:94
  106.7 33.1 %while.54 = (s32[]{:T(128)}, bf16[12416,256]{1,0:T(8,128)(2,1)}, s32[12,2]{0,1:T(2,128)S(1)}, bf16[12,128,256]{2,1,0:T(8,128)(2,1)}, s32[]{:T(128)}) while((s32[]{:T(128)}, bf16[12416,256]{1,0:T(8,128)(2,1)}, s32[12,2]{0,1:T(2,128)S(1)}, bf16[12,128,256]{2,1,0:T(8,128)(2,1)}, s32[]{:T(128)}) %tuple.112), condition=%wide.while_cond.2, body=%wide.while_body.2.sunk | while | flops 2 | bytes 131685 | solution.py:70
  107.2 2.2 bitcast_dynamic-update-slice_fusion.4
  110.0 2.2 bitcast_dynamic-update-slice_fusion.4
  112.8 2.2 bitcast_dynamic-update-slice_fusion.4
  115.5 2.2 bitcast_dynamic-update-slice_fusion.4
  118.3 2.2 bitcast_dynamic-update-slice_fusion.4
  121.1 2.2 bitcast_dynamic-update-slice_fusion.4
  123.8 2.2 bitcast_dynamic-update-slice_fusion.4
  126.6 2.2 bitcast_dynamic-update-slice_fusion.4
  129.3 2.2 bitcast_dynamic-update-slice_fusion.4
  132.1 2.2 bitcast_dynamic-update-slice_fusion.4
  134.8 2.2 bitcast_dynamic-update-slice_fusion.4
  137.6 2.2 bitcast_dynamic-update-slice_fusion.4
  139.8 51.8 %while.55 = (s32[]{:T(128)}, bf16[12416,256]{1,0:T(8,128)(2,1)}, s32[24,2]{0,1:T(2,128)S(1)}, bf16[24,128,256]{2,1,0:T(8,128)(2,1)S(1)}, s32[]{:T(128)}) while((s32[]{:T(128)}, bf16[12416,256]{1,0:T(8,128)(2,1)}, s32[24,2]{0,1:T(2,128)S(1)}, bf16[24,128,256]{2,1,0:T(8,128)(2,1)S(1)}, s32[]{:T(128)}) %tuple.131), condition=%wide.while_cond.3, body=%wide.while_body.3.sunk | while | flops 2 | bytes 131177 | solution.py:70
  140.4 1.6 bitcast_dynamic-update-slice_fusion.5
  142.5 1.6 bitcast_dynamic-update-slice_fusion.5
  144.7 1.6 bitcast_dynamic-update-slice_fusion.5
  146.8 1.6 bitcast_dynamic-update-slice_fusion.5
  149.0 1.6 bitcast_dynamic-update-slice_fusion.5
  151.1 1.6 bitcast_dynamic-update-slice_fusion.5
  153.3 1.6 bitcast_dynamic-update-slice_fusion.5
  155.5 1.6 bitcast_dynamic-update-slice_fusion.5
  157.6 1.6 bitcast_dynamic-update-slice_fusion.5
  159.8 1.6 bitcast_dynamic-update-slice_fusion.5
  161.9 1.6 bitcast_dynamic-update-slice_fusion.5
  164.1 1.6 bitcast_dynamic-update-slice_fusion.5
  166.3 1.6 bitcast_dynamic-update-slice_fusion.5
  168.4 1.6 bitcast_dynamic-update-slice_fusion.5
  170.6 1.6 bitcast_dynamic-update-slice_fusion.5
  172.7 1.6 bitcast_dynamic-update-slice_fusion.5
  174.9 1.6 bitcast_dynamic-update-slice_fusion.5
  177.1 1.6 bitcast_dynamic-update-slice_fusion.5
  179.2 1.6 bitcast_dynamic-update-slice_fusion.5
  181.4 1.6 bitcast_dynamic-update-slice_fusion.5
  183.5 1.6 bitcast_dynamic-update-slice_fusion.5
  185.7 1.6 bitcast_dynamic-update-slice_fusion.5
  187.9 1.6 bitcast_dynamic-update-slice_fusion.5
  190.0 1.6 bitcast_dynamic-update-slice_fusion.5
  193.3 1.5 dot_general.23
  195.3 5.4 %fusion.29 = f32[256,3072]{1,0:T(8,128)S(1)} fusion(bf16[1536,256]{1,0:T(8,128)(2,1)S(1)} %bitcast.62, bf16[3072,1536]{1,0:T(8,128)(2,1)} %param.8), kind=kOutput, calls=%fused_computation.51 | convolution fusion | flops 2415919104 | bytes 13369344 | tf_op jit(solution)/shard_map/dot_general | solution.py:104
  200.7 2.6 fusion.17
  203.3 8.6 %all_to_all.25 = f32[4,32,2,256]{3,1,2,0:T(8,128)S(1)} all-to-all(f32[4,32,2,256]{3,1,2,0:T(8,128)S(1)} %fusion.17), channel_id=1, replica_groups=mesh['sib'=2,'row'=8,'col_0'=4,'col_1'=4] {'col_1'}, dimensions={0} | all-to-all | bytes 524288 | tf_op jit(solution)/shard_map/all_to_all | solution.py:44
  211.9 19.4 %all_to_all.26 = f32[32,2,256]{2,1,0:T(2,128)S(1)} all-to-all(f32[32,2,256]{2,1,0:T(2,128)S(1)} %copy.19), channel_id=1, replica_groups=mesh['sib'=2,'row'=8,'col_0'=4,'col_1'=4] {'row','col_0'}, dimensions={0} | all-to-all | bytes 131072 | tf_op jit(solution)/shard_map/all_to_all | solution.py:52
  231.4 13.1 %all_to_all.27 = f32[32,2,256]{2,1,0:T(2,128)S(1)} all-to-all(f32[32,2,256]{2,1,0:T(2,128)S(1)} %broadcast_in_dim.34), channel_id=1, replica_groups=mesh['sib'=2,'row'=8,'col_0'=4,'col_1'=4] {'row','col_0'}, dimensions={0} | all-to-all | bytes 131072 | tf_op jit(solution)/shard_map/all_to_all | solution.py:20
  245.3 6.1 %all-to-all-start.4 = ((f32[4,32,2,256]{3,2,1,0:T(2,128)}), f32[4,32,2,256]{3,2,1,0:T(2,128)S(1)}, u32[]{:S(2)}, u32[]{:S(2)}) async-start(f32[4,32,2,256]{3,2,1,0:T(2,128)} %broadcast_in_dim.35), calls=%async_computation.4 | async-start | bytes 524288 | tf_op jit(solution)/shard_map/all_to_all | solution.py:20
  251.3 2.3 copy.16
  255.1 8.2 %all-to-all-start = ((f32[16,192,256]{2,1,0:T(8,128)}), f32[16,192,256]{2,1,0:T(8,128)S(1)}, u32[]{:S(2)}, u32[]{:S(2)}) async-start(f32[16,192,256]{2,1,0:T(8,128)} %bitcast.7), calls=%async_computation | async-start | bytes 6291456 | tf_op jit(solution)/shard_map/all_to_all | solution.py:44
  266.1 1.7 add.118
  267.8 33.8 %all-to-all-done = f32[16,192,256]{2,1,0:T(8,128)S(1)} async-done(((f32[16,192,256]{2,1,0:T(8,128)}), f32[16,192,256]{2,1,0:T(8,128)S(1)}, u32[]{:S(2)}, u32[]{:S(2)}) %all-to-all-start) | async-done | bytes 3145760 | tf_op jit(solution)/shard_map/all_to_all | solution.py:44
  (321 shorter events, 106.3 us)
Async XLA Ops:
  7.2 93.0 %all-gather.2.cloned.1.call-start = ((), (), s32[]{:S(2)}) async-start(), calls=%async_computation.5 | async-start | bytes 6684672 | tf_op jit(solution)/shard_map/all_gather | solution.py:93
  193.3 1.5 copy-start.1
  195.3 5.4 %copy-start = (bf16[32,4,2,3072]{3,2,1,0:T(2,128)(2,1)S(1)}, bf16[32,4,2,3072]{3,2,1,0:T(2,128)(2,1)}, u32[]{:S(2)}) copy-start(bf16[32,4,2,3072]{3,2,1,0:T(2,128)(2,1)} %dot_general.23) | copy-start | bytes 4718596
  245.3 9.8 %all-to-all-start.4 = ((f32[4,32,2,256]{3,2,1,0:T(2,128)}), f32[4,32,2,256]{3,2,1,0:T(2,128)S(1)}, u32[]{:S(2)}, u32[]{:S(2)}) async-start(f32[4,32,2,256]{3,2,1,0:T(2,128)} %broadcast_in_dim.35), calls=%async_computation.4 | async-start | bytes 524288 | tf_op jit(solution)/shard_map/all_to_all | solution.py:20
  255.1 46.6 %all-to-all-start = ((f32[16,192,256]{2,1,0:T(8,128)}), f32[16,192,256]{2,1,0:T(8,128)S(1)}, u32[]{:S(2)}, u32[]{:S(2)}) async-start(f32[16,192,256]{2,1,0:T(8,128)} %bitcast.7), calls=%async_computation | async-start | bytes 6291456 | tf_op jit(solution)/shard_map/all_to_all | solution.py:44
Sparse Core Ops, SparseCore 0:
  10.4 67.4 all-gather.1
where the time goes:
time: 314 us; the launch traced here: 309 us
  local copies, waits for them, and re-layouts  189 us (60%)
  blocking collectives  41.1 us (13%)
  waiting for transfers between devices  35.9 us (11%)
  starting transfers between devices  14.3 us (5%)
  between operations  14.3 us (5%)
  matrix products  9.23 us (3%)
  other arithmetic  4.64 us (1%)
    gather x216, local copies, waits for them, and re-layouts  132 us
    gather x28, local copies, waits for them, and re-layouts, spread_range(): first = jnp.searchsorted(places, starts)  41.4 us
    all_to_all x1, waiting for transfers between devices, sum_at_owner(): tiles = lax.all_to_all(cut_along(x, dim, count), axis, 0, 0, tiled=True)  33.8 us
    all_to_all x1, blocking collectives, sum_in_two_steps(): lax.all_to_all(nearer, far, split_axis=0, concat_axis=0, tiled=True)  19.4 us
    all_to_all x1, blocking collectives, copy_for_each(): lax.all_to_all(jnp.broadcast_to(x[None], (count, *x.shape)), axis, 0, 0,...  13.1 us
    all_to_all x1, blocking collectives, sum_at_owner(): tiles = lax.all_to_all(cut_along(x, dim, count), axis, 0, 0, tiled=True)  8.59 us
    all_to_all x1, starting transfers between devices, sum_at_owner(): tiles = lax.all_to_all(cut_along(x, dim, count), axis, 0, 0, tiled=True)  8.2 us
    concatenate x1, local copies, waits for them, and re-layouts, shards(): jnp.concatenate([whole_panel, jnp.zeros((128, width), jnp.bfloat16)], axi...  6.45 us
  transfers between devices with their start and end apart: 3, of which 2 were waited for; matrix products, arithmetic and copies ran while one was open for 32% of the time, Pallas kernels for 0%

commit v1 on v0

v1 whole, which is shorter than its diff:
```python
import functools

import jax
import jax.numpy as jnp
from jax import lax
from jax.experimental import pallas as pl
from jax.experimental.pallas import tpu as pltpu
from jax.sharding import Mesh
from jax.sharding import PartitionSpec as P

COL = ("col_0", "col_1")
ROW_COL = ("row", "col_0", "col_1")
MESH_ID = pl.DeviceIdType.MESH
LANES = 128
GROUP = 16
SIDE = 4
SPAN = 8
F32 = jnp.float32
BF16 = jnp.bfloat16


def kernel(
    panel, places, front, dinv, off_out, diag_out,
    gath, wind, spread, front_v, part, ring_1, mid, ring_2, own_s, hits,
    terms, got_d, sum_z, got_z, total,
    send, rg, rz, r1, r2, rs, rd, rzz, rt, loc,
):
    nblk = panel.shape[0]
    nchunk = places.shape[0]
    front_rows, front_cols = front.shape
    ntgt = front_cols // LANES
    nwin = wind.shape[1]
    own = own_s.shape[0]
    z = lax.axis_index("row")
    pos = {"col_0": lax.axis_index("col_0"), "col_1": lax.axis_index("col_1")}
    px, py = pos["col_0"], pos["col_1"]
    col = px * SIDE + py
    order = (("col_0", "col_1"), ("col_1", "col_0"))
    sends = []

    def put(src, dst, sem, **device):
        copy = pltpu.make_async_remote_copy(
            src_ref=src, dst_ref=dst, send_sem=send.at[len(sends)], recv_sem=sem,
            device_id=device, device_id_type=MESH_ID,
        )
        copy.start()
        sends.append(copy)

    def arrive(dst, sem):
        pltpu.make_async_copy(dst, dst, sem).wait()

    def step(axis, delta):
        return {axis: lax.rem(pos[axis] + delta + SIDE, SIDE)}

    def in_plane(off):
        peer = lax.rem(col + off, SIDE * SIDE)
        return peer, {"col_0": peer // SIDE, "col_1": lax.rem(peer, SIDE)}

    to_row = col // 2
    to_col = SPAN * lax.rem(col, 2) + z
    from_col = 2 * z + col // SPAN
    from_row = lax.rem(col, SPAN)
    stays = jnp.logical_and(to_row == z, to_col == col)
    goes = jnp.logical_not(stays)
    to_dev = {"row": to_row, "col_0": to_col // SIDE, "col_1": lax.rem(to_col, SIDE)}
    from_dev = {"row": from_row, "col_0": from_col // SIDE, "col_1": lax.rem(from_col, SIDE)}

    load_front = pltpu.make_async_copy(front, front_v, loc.at[0])
    load_front.start()

    barrier = pltpu.get_barrier_semaphore()
    for off in range(1, SIDE * SIDE):
        pl.semaphore_signal(barrier, inc=1, device_id=in_plane(off)[1], device_id_type=MESH_ID)
    for off in range(1, SPAN):
        pl.semaphore_signal(
            barrier, inc=1, device_id={"row": lax.rem(z + off, SPAN)}, device_id_type=MESH_ID
        )

    @pl.when(goes)
    def _():
        pl.semaphore_signal(barrier, inc=1, device_id=to_dev, device_id_type=MESH_ID)
        pl.semaphore_signal(barrier, inc=1, device_id=from_dev, device_id_type=MESH_ID)

    pl.semaphore_wait(barrier, SIDE * SIDE - 1 + SPAN - 1 + 2 * goes.astype(jnp.int32))

    def slot(h, d0, d1):
        a0, a1 = order[h]
        c0 = lax.rem(pos[a0] + d0, SIDE)
        c1 = lax.rem(pos[a1] + d1, SIDE)
        k = c0 * SIDE + c1 if h == 0 else c1 * SIDE + c0
        return gath.at[h, pl.ds(k * nblk, nblk)]

    def mine(h):
        return panel.at[:, z, :, pl.ds(h * LANES, LANES)]

    def pass_on(h, d0, d1, which, delta, src=None):
        dst = slot(h, d0, d1)
        d0, d1 = ((d0 - delta) % SIDE, d1) if which == 0 else (d0, (d1 - delta) % SIDE)
        put(dst if src is None else src, dst, rg.at[h, d0, d1], **step(order[h][which], delta))

    def gathered(h, d0, d1):
        arrive(slot(h, d0, d1), rg.at[h, d0, d1])

    for h in range(2):
        for delta in (1, -1, 2):
            pass_on(h, 0, 0, 0, delta, mine(h))
        for delta in (1, -1):
            pass_on(h, 0, 0, 1, delta, mine(h))
    keep = [pltpu.make_async_copy(mine(h), slot(h, 0, 0), loc.at[1 + h]) for h in range(2)]
    for copy in keep:
        copy.start()

    place = places[...]

    def chunk_of(bound):
        return jnp.sum((place < bound).astype(jnp.int32)) // LANES

    col_base = col * front_cols
    chunks = [chunk_of(col_base + t * LANES) for t in range(ntgt)]
    first = jnp.minimum(chunks[0], nchunk - nwin)
    own_base = z * front_rows + col * own
    nown = hits.shape[0]
    own_first = jnp.minimum(chunk_of(own_base), nchunk - nown)
    target = lax.broadcasted_iota(jnp.int32, (own, LANES), 0) + own_base
    mark = jnp.zeros((own, LANES), F32)
    for i in range(nown):
        mark += jnp.where(places[pl.ds(own_first + i, 1), :] == target, 1.0, 0.0)
    hit_rows = jnp.broadcast_to(jnp.max(mark, axis=1, keepdims=True), (own, LANES))
    hits[0] = hit_rows

    for d in (1, 3):
        for h in range(2):
            gathered(h, d, 0)
            pass_on(h, d, 0, 1, 1)
            pass_on(h, d, 0, 1, -1)
    for h in range(2):
        gathered(h, 0, 3)
        pass_on(h, 0, 3, 1, 1)
    for h in range(2):
        gathered(h, 2, 0)
        pass_on(h, 2, 0, 1, 1)
        pass_on(h, 2, 0, 1, -1)
    for h in range(2):
        gathered(h, 1, 3)
        pass_on(h, 1, 3, 1, 1)
        gathered(h, 3, 1)
        pass_on(h, 3, 1, 1, -1)
    for h in range(2):
        gathered(h, 2, 1)
        pass_on(h, 2, 1, 1, -1)
    for copy in keep:
        copy.wait()
    for h in range(2):
        for d in ((0, 1), (2, 3), (3, 3), (1, 1), (0, 2), (1, 2), (2, 2), (3, 2)):
            gathered(h, *d)

    for h in range(2):
        for i in range(nwin):
            wind[h, i, z] = gath[h, first + i]

    def share(h, d):
        return wind.at[h, :, lax.rem(z + d + SPAN, SPAN)]

    last = ((SPAN // 2, SPAN // 2 - 1), (SPAN // 2 - 1, SPAN // 2))
    for s in range(1, SPAN // 2 + 1):
        for h in range(2):
            for d, sign in enumerate((1, -1)):
                if s <= last[h][d]:
                    if s > 1:
                        arrive(share(h, -sign * (s - 1)), rz.at[h, d, s - 2])
                    block = share(h, -sign * (s - 1))
                    put(block, block, rz.at[h, d, s - 1], row=lax.rem(z + sign + SPAN, SPAN))
    for h in range(2):
        for d, sign in enumerate((1, -1)):
            arrive(share(h, -sign * last[h][d]), rz.at[h, d, last[h][d] - 1])

    rows_at = lax.broadcasted_iota(jnp.int32, (LANES, LANES), 0)
    for t in range(ntgt):
        a = jnp.minimum(chunks[t] - first, nwin - 2)
        want = rows_at + (col_base + t * LANES)
        table = jnp.concatenate(
            [
                jnp.where(places[pl.ds(first + a + i, 1), :] == want, 1.0, 0.0).astype(BF16)
                for i in range(2)
            ],
            axis=1,
        )
        for h in range(2):
            rows = wind[h, pl.ds(a, 2)].reshape(2 * LANES, LANES)
            spread[pl.ds(t * LANES, LANES), pl.ds(h * LANES, LANES)] = jnp.dot(
                table, rows, preferred_element_type=F32
            ).astype(BF16)

    given = spread.at[pl.ds(pl.multiple_of(z * own, GROUP), own)]
    give = pltpu.make_async_remote_copy(
        src_ref=given, dst_ref=own_s, send_sem=loc.at[3], recv_sem=rs,
        device_id=to_dev, device_id_type=MESH_ID,
    )

    @pl.when(goes)
    def _():
        give.start()

    @pl.when(stays)
    def _():
        copy = pltpu.make_async_copy(given, own_s, loc.at[4])
        copy.start()
        copy.wait()

    def near(h, d, j, src=None):
        put(part.at[h, 1 if d == 0 else 3, j], ring_1.at[h, d, j], r1.at[h, d, j],
            **step(order[h][0], 1 - 2 * d))

    def far(h, d, j):
        at = SIDE + j % 2
        put(part.at[h, 2, j], ring_1.at[h, d, at], r1.at[h, d, at], **step(order[h][0], 1 - 2 * d))

    load_front.wait()
    stripe = SIDE * own
    for d in (2, 1, 3, 0):
        at = pl.multiple_of(lax.rem(px + d, SIDE) * stripe, stripe)
        block = jnp.dot(
            front_v[pl.ds(at, stripe), :], spread[...], preferred_element_type=F32
        )
        for y in range(SIDE):
            j = lax.rem(y - py + SIDE, SIDE)
            part[0, d, j] = block[y * own:(y + 1) * own, :LANES]
            part[1, j, d] = block[y * own:(y + 1) * own, LANES:]
        if d == 2:
            for j in range(SIDE):
                far(0, j // 2, j)
        if d == 1:
            near(0, 0, 2)
            near(0, 0, 3)
        if d == 3:
            near(0, 1, 0)
            near(0, 1, 1)
        far(1, d // 2, d)
        near(1, 0 if d >= 2 else 1, d)
    for jj in range(2):
        for h in range(2):
            for d in range(2):
                j = 2 * d + jj
                arrive(ring_1.at[h, d, SIDE + jj], r1.at[h, d, SIDE + jj])
                at = 1 if d == 0 else 3
                part[h, at, j] = part[h, at, j] + ring_1[h, d, SIDE + jj]
                near(h, d, j)

    half = own // 2

    def near_2(h, d, u):
        put(mid.at[h, 1 if d == 0 else 3, u], ring_2.at[h, d, u], r2.at[h, d, u],
            **step(order[h][1], 1 - 2 * d))

    for j in (2, 1, 3, 0):
        for h in range(2):
            for d in range(2):
                arrive(ring_1.at[h, d, j], r1.at[h, d, j])
            both = part[h, 0, j] + ring_1[h, 0, j] + ring_1[h, 1, j]
            mid[h, j, 0] = both[:half]
            mid[h, j, 1] = both[half:]
            if j == 2:
                for d in range(2):
                    put(mid.at[h, 2, d], ring_2.at[h, d, 2], r2.at[h, d, 2],
                        **step(order[h][1], 1 - 2 * d))
            if j == 1:
                near_2(h, 0, 1)
            if j == 3:
                near_2(h, 1, 0)
    for h in range(2):
        for d in range(2):
            arrive(ring_2.at[h, d, 2], r2.at[h, d, 2])
            at = 1 if d == 0 else 3
            mid[h, at, d] = mid[h, at, d] + ring_2[h, d, 2]
            near_2(h, d, d)
    halves = []
    for h in range(2):
        both = []
        for u in range(2):
            for d in range(2):
                arrive(ring_2.at[h, d, u], r2.at[h, d, u])
            both.append(mid[h, 0, u] + ring_2[h, 0, u] + ring_2[h, 1, u])
        halves.append(jnp.concatenate(both, axis=0))
    hit_rows = hits[0]
    for h in range(2):
        off_out[:, pl.ds(h * LANES, LANES)] = jnp.where(hit_rows > 0.5, -halves[h], 0.0)
    product = jnp.concatenate(halves, axis=1)

    @pl.when(goes)
    def _():
        give.wait()

    high = product.astype(BF16)
    low = (product - high.astype(F32)).astype(BF16)
    rows = own_s[...]
    dims = (((0,), (0,)), ((), ()))
    here = lax.dot_general(rows, high, dims, preferred_element_type=F32)
    here += lax.dot_general(rows, low, dims, preferred_element_type=F32)
    terms[...] = here.reshape(terms.shape)
    for off in range(1, SIDE * SIDE):
        peer, device = in_plane(off)
        put(terms.at[peer], got_d.at[off - 1], rd.at[off - 1], **device)
    acc = terms[col]
    for off in range(1, SIDE * SIDE):
        arrive(got_d.at[off - 1], rd.at[off - 1])
        acc += got_d[off - 1]
    sum_z[...] = acc
    for off in range(1, SPAN):
        put(sum_z, got_z.at[off - 1], rzz.at[off - 1], row=lax.rem(z + off, SPAN))
    for off in range(1, SPAN):
        arrive(got_z.at[off - 1], rzz.at[off - 1])
    acc = jnp.zeros_like(acc)
    got_z[SPAN - 1] = sum_z[...]
    for r in range(SPAN):
        at = lax.rem(z - r + SPAN - 1 + SPAN, SPAN)
        acc += got_z[at]
    total[col] = acc
    for off in range(1, SIDE * SIDE):
        peer, device = in_plane(off)
        put(total.at[col], total.at[col], rt.at[off - 1], **device)
    for off in range(1, SIDE * SIDE):
        peer = lax.rem(col - off + SIDE * SIDE, SIDE * SIDE)
        arrive(total.at[peer], rt.at[off - 1])
    diag_out[...] = dinv[...] + total[...].reshape(dinv.shape)
    for copy in sends:
        copy.wait_send()


def shards(front_inverse, panel, row_map, diag_inverse):
    front_rows, front_cols = front_inverse.shape
    _, block, width = panel.shape
    count = row_map.shape[1]
    nchunk = count // LANES
    nwin = front_cols // LANES + 1
    own = front_rows // (SIDE * SIDE)
    nown = (own + 2 * LANES - 2) // LANES
    slab = width // (SIDE * SIDE)
    vmem = pltpu.VMEM
    dma = pltpu.SemaphoreType.DMA
    offdiag, diag = pl.pallas_call(
        kernel,
        out_shape=(
            jax.ShapeDtypeStruct((own, width), F32),
            jax.ShapeDtypeStruct((width, width), F32),
        ),
        in_specs=[
            pl.BlockSpec(memory_space=pl.ANY),
            pl.BlockSpec(memory_space=pltpu.VMEM),
            pl.BlockSpec(memory_space=pl.ANY),
            pl.BlockSpec(memory_space=pltpu.VMEM),
        ],
        out_specs=(
            pl.BlockSpec(memory_space=pltpu.VMEM),
            pl.BlockSpec(memory_space=pltpu.VMEM),
        ),
        scratch_shapes=[
            vmem((2, nchunk, GROUP, LANES), BF16),
            vmem((2, nwin, SPAN, GROUP, LANES), BF16),
            vmem((front_cols, width), BF16),
            vmem((front_rows, front_cols), BF16),
            vmem((2, SIDE, SIDE, own, LANES), F32),
            vmem((2, 2, SIDE + 2, own, LANES), F32),
            vmem((2, SIDE, 2, own // 2, LANES), F32),
            vmem((2, 2, 3, own // 2, LANES), F32),
            vmem((own, width), BF16),
            vmem((nown, own, LANES), F32),
            vmem((SIDE * SIDE, slab, width), F32),
            vmem((SIDE * SIDE - 1, slab, width), F32),
            vmem((slab, width), F32),
            vmem((SPAN, slab, width), F32),
            vmem((SIDE * SIDE, slab, width), F32),
            dma((160,)),
            dma((2, SIDE, SIDE)),
            dma((2, 2, SPAN // 2)),
            dma((2, 2, SIDE + 2)),
            dma((2, 2, 3)),
            dma,
            dma((SIDE * SIDE - 1,)),
            dma((SPAN - 1,)),
            dma((SIDE * SIDE - 1,)),
            dma((5,)),
        ],
        compiler_params=pltpu.CompilerParams(
            collective_id=0, has_side_effects=True, vmem_limit_bytes=60 * 1024 * 1024
        ),
        name="selected_inverse",
    )(
        panel.reshape(block // (SPAN * GROUP), SPAN, GROUP, width),
        row_map.reshape(nchunk, LANES),
        front_inverse,
        diag_inverse[0],
    )
    return offdiag[None], diag[None]


def solution(mesh):
    finer = Mesh(
        mesh.devices.reshape(mesh.shape["sib"], mesh.shape["row"], SIDE, SIDE),
        ("sib", "row", "col_0", "col_1"),
    )
    return jax.shard_map(
        shards,
        mesh=finer,
        in_specs=(P("row", COL), P("sib", COL, None), P("sib", None), P("sib", None, None)),
        out_specs=(P("sib", ROW_COL, None), P("sib", None, None)),
        check_vma=False,
    )
```

time: 314 us -> 87.3 us (0.28)
  the two profiles are of different devices: /device:TPU:20 before, /device:TPU:32 now
where the time goes in v1:
time: 87.3 us; the launch traced here: 86.7 us
  Pallas kernels  82.8 us (95%)
  local copies, waits for them, and re-layouts  3.29 us (4%)
    pallas_call x1, Pallas kernels, shards(): pl.pallas_call(kernel, out_shape=(jax.ShapeDtypeStruct((own, width), F32)...  82.8 us
    unnamed x2, local copies, waits for them, and re-layouts  3.29 us

profile of v1, /device:TPU:32, one launch (start us, length us, event | category | flops | bytes accessed | tf_op | source)
XLA Modules:
  0.0 86.7 jit_solution(5802135999615240863)
XLA Ops:
  0.6 82.8 %selected_inverse.1 = (f32[192,256]{1,0:T(8,128)}, f32[256,256]{1,0:T(8,128)}) custom-call(bf16[6,8,16,256]{3,2,1,0:T(8,128)(2,1)} %bitcast.5, s32[96,128]{1,0:T(8,128)} %bitcast.9, bf16[3072,1536]{1,0:T(8,128)(2,1)} %front.1, f32[256,256]{1,0:T(8,128)} %bitcast.6), custom_call_target="tpu_custom_call" | custom-call | tf_op jit(solution)/shard_map/selected_inverse/pallas_call | solution.py:340
  83.4 1.6 %copy.8 = f32[1,192,256]{2,1,0:T(8,128)} copy(f32[1,192,256]{2,1,0:T(8,128)} %bitcast.8) | data formatting | bytes 393216
  85.0 1.7 %copy.9 = f32[1,256,256]{2,1,0:T(8,128)} copy(f32[1,256,256]{2,1,0:T(8,128)} %bitcast.7) | data formatting | bytes 524288

commit v2 on v1

--- a/solution.py
+++ b/solution.py
@@ -13,6 +13,8 @@
 MESH_ID = pl.DeviceIdType.MESH
 LANES = 128
 GROUP = 16
+LEVELS = 32767.0
+TINY = 1e-33
 SIDE = 4
 SPAN = 8
 F32 = jnp.float32
@@ -21,7 +23,7 @@
 
 def kernel(
     panel, places, front, dinv, off_out, diag_out,
-    gath, wind, spread, front_v, part, ring_1, mid, ring_2, own_s, hits,
+    gath, wind, spread, front_v, part, out_1, ring_1, mid, out_2, ring_2, scale, own_s, hits,
     terms, got_d, sum_z, got_z, total,
     send, rg, rz, r1, r2, rs, rd, rzz, rt, loc,
 ):
@@ -69,19 +71,17 @@
     load_front.start()
 
     barrier = pltpu.get_barrier_semaphore()
-    for off in range(1, SIDE * SIDE):
-        pl.semaphore_signal(barrier, inc=1, device_id=in_plane(off)[1], device_id_type=MESH_ID)
-    for off in range(1, SPAN):
+    for axis in ("col_0", "col_1"):
+        for delta in (1, -1, 2):
+            pl.semaphore_signal(
+                barrier, inc=1, device_id=step(axis, delta), device_id_type=MESH_ID
+            )
+    for delta in (1, -1):
         pl.semaphore_signal(
-            barrier, inc=1, device_id={"row": lax.rem(z + off, SPAN)}, device_id_type=MESH_ID
+            barrier, inc=1, device_id={"row": lax.rem(z + delta + SPAN, SPAN)},
+            device_id_type=MESH_ID,
         )
-
-    @pl.when(goes)
-    def _():
-        pl.semaphore_signal(barrier, inc=1, device_id=to_dev, device_id_type=MESH_ID)
-        pl.semaphore_signal(barrier, inc=1, device_id=from_dev, device_id_type=MESH_ID)
-
-    pl.semaphore_wait(barrier, SIDE * SIDE - 1 + SPAN - 1 + 2 * goes.astype(jnp.int32))
+    pl.semaphore_wait(barrier, 2 * (SIDE - 1) + 2)
 
     def slot(h, d0, d1):
         a0, a1 = order[h]
@@ -207,13 +207,30 @@
         copy.start()
         copy.wait()
 
-    def near(h, d, j, src=None):
-        put(part.at[h, 1 if d == 0 else 3, j], ring_1.at[h, d, j], r1.at[h, d, j],
-            **step(order[h][0], 1 - 2 * d))
+    def post(value, out, dst, at, sem, device):
+        top = jnp.maximum(jnp.max(jnp.abs(value), axis=0, keepdims=True), TINY)
+        out[...] = jnp.round(value * (LEVELS / top)).astype(jnp.int32).astype(jnp.int16)
+        scale[(0, *at)] = top * (1.0 / LEVELS)
+        put(scale.at[(0, *at)], scale.at[(1, *at)], sem.at[(1, *at[1:])], **device)
+        put(out, dst, sem.at[(0, *at[1:])], **device)
+
+    def fetch(dst, at, sem):
+        arrive(scale.at[(1, *at)], sem.at[(1, *at[1:])])
+        arrive(dst, sem.at[(0, *at[1:])])
+        return dst[...].astype(jnp.int32).astype(F32) * scale[(1, *at)]
+
+    def post_1(value, h, d, at):
+        post(value, out_1.at[h, d, at], ring_1.at[h, d, at], (0, h, d, at), r1,
+             step(order[h][0], 1 - 2 * d))
+
+    def fetch_1(h, d, at):
+        return fetch(ring_1.at[h, d, at], (0, h, d, at), r1)
+
+    def near(h, d, j):
+        post_1(part[h, 1 if d == 0 else 3, j], h, d, j)
 
     def far(h, d, j):
-        at = SIDE + j % 2
-        put(part.at[h, 2, j], ring_1.at[h, d, at], r1.at[h, d, at], **step(order[h][0], 1 - 2 * d))
+        post_1(part[h, 2, j], h, d, SIDE + j % 2)
 
     load_front.wait()
     stripe = SIDE * own
@@ -241,45 +258,38 @@
         for h in range(2):
             for d in range(2):
                 j = 2 * d + jj
-                arrive(ring_1.at[h, d, SIDE + jj], r1.at[h, d, SIDE + jj])
-                at = 1 if d == 0 else 3
-                part[h, at, j] = part[h, at, j] + ring_1[h, d, SIDE + jj]
-                near(h, d, j)
+                post_1(part[h, 1 if d == 0 else 3, j] + fetch_1(h, d, SIDE + jj), h, d, j)
 
     half = own // 2
 
-    def near_2(h, d, u):
-        put(mid.at[h, 1 if d == 0 else 3, u], ring_2.at[h, d, u], r2.at[h, d, u],
-            **step(order[h][1], 1 - 2 * d))
+    def post_2(value, h, d, at):
+        post(value, out_2.at[h, d, at], ring_2.at[h, d, at], (1, h, d, at), r2,
+             step(order[h][1], 1 - 2 * d))
+
+    def fetch_2(h, d, at):
+        return fetch(ring_2.at[h, d, at], (1, h, d, at), r2)
 
     for j in (2, 1, 3, 0):
         for h in range(2):
-            for d in range(2):
-                arrive(ring_1.at[h, d, j], r1.at[h, d, j])
-            both = part[h, 0, j] + ring_1[h, 0, j] + ring_1[h, 1, j]
-            mid[h, j, 0] = both[:half]
-            mid[h, j, 1] = both[half:]
+            both = part[h, 0, j] + fetch_1(h, 0, j) + fetch_1(h, 1, j)
             if j == 2:
                 for d in range(2):
-                    put(mid.at[h, 2, d], ring_2.at[h, d, 2], r2.at[h, d, 2],
-                        **step(order[h][1], 1 - 2 * d))
+                    post_2(both[d * half:(d + 1) * half], h, d, 2)
+            else:
+                mid[h, j // 2 if j else 2] = both
             if j == 1:
-                near_2(h, 0, 1)
+                post_2(both[half:], h, 0, 1)
             if j == 3:
-                near_2(h, 1, 0)
+                post_2(both[:half], h, 1, 0)
     for h in range(2):
         for d in range(2):
-            arrive(ring_2.at[h, d, 2], r2.at[h, d, 2])
-            at = 1 if d == 0 else 3
-            mid[h, at, d] = mid[h, at, d] + ring_2[h, d, 2]
-            near_2(h, d, d)
+            post_2(mid[h, d, pl.ds(d * half, half)] + fetch_2(h, d, 2), h, d, d)
     halves = []
     for h in range(2):
         both = []
         for u in range(2):
-            for d in range(2):
-                arrive(ring_2.at[h, d, u], r2.at[h, d, u])
-            both.append(mid[h, 0, u] + ring_2[h, 0, u] + ring_2[h, 1, u])
+            rows = mid[h, 2, pl.ds(u * half, half)]
+            both.append(rows + fetch_2(h, 0, u) + fetch_2(h, 1, u))
         halves.append(jnp.concatenate(both, axis=0))
     hit_rows = hits[0]
     for h in range(2):
@@ -326,6 +336,11 @@
         copy.wait_send()
 
 
+def finish(off, diag, off_out, diag_out):
+    off_out[...] = off[...]
+    diag_out[...] = diag[...]
+
+
 def shards(front_inverse, panel, row_map, diag_inverse):
     front_rows, front_cols = front_inverse.shape
     _, block, width = panel.shape
@@ -359,9 +374,12 @@
             vmem((front_cols, width), BF16),
             vmem((front_rows, front_cols), BF16),
             vmem((2, SIDE, SIDE, own, LANES), F32),
-            vmem((2, 2, SIDE + 2, own, LANES), F32),
-            vmem((2, SIDE, 2, own // 2, LANES), F32),
-            vmem((2, 2, 3, own // 2, LANES), F32),
+            vmem((2, 2, SIDE + 2, own, LANES), jnp.int16),
+            vmem((2, 2, SIDE + 2, own, LANES), jnp.int16),
+            vmem((2, 3, own, LANES), F32),
+            vmem((2, 2, 3, own // 2, LANES), jnp.int16),
+            vmem((2, 2, 3, own // 2, LANES), jnp.int16),
+            vmem((2, 2, 2, 2, SIDE + 2, 1, LANES), F32),
             vmem((own, width), BF16),
             vmem((nown, own, LANES), F32),
             vmem((SIDE * SIDE, slab, width), F32),
@@ -372,8 +390,8 @@
             dma((160,)),
             dma((2, SIDE, SIDE)),
             dma((2, 2, SPAN // 2)),
-            dma((2, 2, SIDE + 2)),
-            dma((2, 2, 3)),
+            dma((2, 2, 2, SIDE + 2)),
+            dma((2, 2, 2, 3)),
             dma,
             dma((SIDE * SIDE - 1,)),
             dma((SPAN - 1,)),
@@ -390,6 +408,17 @@
         front_inverse,
         diag_inverse[0],
     )
+    whole = pl.BlockSpec(memory_space=pltpu.VMEM)
+    offdiag, diag = pl.pallas_call(
+        finish,
+        out_shape=(
+            jax.ShapeDtypeStruct((own, width), F32),
+            jax.ShapeDtypeStruct((width, width), F32),
+        ),
+        in_specs=[whole, whole],
+        out_specs=(whole, whole),
+        name="outputs",
+    )(offdiag, diag)
     return offdiag[None], diag[None]
 
 

time: 87.3 us -> 80.9 us (0.927)
  local copies, waits for them, and re-layouts: 3.29 us -> 0 us
  Pallas kernels: 82.8 us -> 80.2 us
    pallas_call x1, Pallas kernels: 82.8 us -> 78.4 us  [shards(): pl.pallas_call(kernel, out_shape=(jax.ShapeDtypeStruct((own, width), F32)...]
    unnamed x2 -> x0, local copies, waits for them, and re-layouts: 3.29 us -> none
    pallas_call x0 -> x1, Pallas kernels: none -> 1.84 us  [shards(): pl.pallas_call(finish, out_shape=(jax.ShapeDtypeStruct((own, width), F32)...]
where the time goes in v2:
time: 80.9 us; the launch traced here: 80.8 us
  Pallas kernels  80.2 us (99%)
    pallas_call x1, Pallas kernels, shards(): pl.pallas_call(kernel, out_shape=(jax.ShapeDtypeStruct((own, width), F32)...  78.4 us
    pallas_call x1, Pallas kernels, shards(): pl.pallas_call(finish, out_shape=(jax.ShapeDtypeStruct((own, width), F32)...  1.84 us

profile of v2, /device:TPU:32, one launch (start us, length us, event | category | flops | bytes accessed | tf_op | source)
XLA Modules:
  0.0 80.8 jit_solution(3354948903069051602)
XLA Ops:
  0.6 78.4 %selected_inverse.1 = (f32[192,256]{1,0:T(8,128)}, f32[256,256]{1,0:T(8,128)}) custom-call(bf16[6,8,16,256]{3,2,1,0:T(8,128)(2,1)} %bitcast.5, s32[96,128]{1,0:T(8,128)} %bitcast.7, bf16[3072,1536]{1,0:T(8,128)(2,1)} %front.1, f32[256,256]{1,0:T(8,128)} %bitcast.6), custom_call_target="tpu_custom_call" | custom-call | tf_op jit(solution)/shard_map/selected_inverse/pallas_call | solution.py:355
  79.0 1.8 %outputs.1 = (f32[192,256]{1,0:T(8,128)}, f32[256,256]{1,0:T(8,128)}) custom-call(f32[192,256]{1,0:T(8,128)} %get-tuple-element.6.off, f32[256,256]{1,0:T(8,128)} %get-tuple-element.7.diag), custom_call_target="tpu_custom_call" | custom-call | tf_op jit(solution)/shard_map/outputs/pallas_call | solution.py:412

commit v3 on v2

--- a/solution.py
+++ b/solution.py
@@ -22,8 +22,8 @@
 
 
 def kernel(
-    panel, places, front, dinv, off_out, diag_out,
-    gath, wind, spread, front_v, part, out_1, ring_1, mid, out_2, ring_2, scale, own_s, hits,
+    panel, places_in, front, dinv_in, off_out, diag_out,
+    places, dinv, off_v, diag_v, gath, wind, spread, front_v, part, out_1, ring_1, mid, out_2, ring_2, scale, own_s, hits,
     terms, got_d, sum_z, got_z, total,
     send, rg, rz, r1, r2, rs, rd, rzz, rt, loc,
 ):
@@ -31,7 +31,7 @@
     nchunk = places.shape[0]
     front_rows, front_cols = front.shape
     ntgt = front_cols // LANES
-    nwin = wind.shape[1]
+    nwin = wind.shape[2]
     own = own_s.shape[0]
     z = lax.axis_index("row")
     pos = {"col_0": lax.axis_index("col_0"), "col_1": lax.axis_index("col_1")}
@@ -55,8 +55,11 @@
         return {axis: lax.rem(pos[axis] + delta + SIDE, SIDE)}
 
     def in_plane(off):
-        peer = lax.rem(col + off, SIDE * SIDE)
-        return peer, {"col_0": peer // SIDE, "col_1": lax.rem(peer, SIDE)}
+        x, y = lax.rem(px + off // SIDE, SIDE), lax.rem(py + off % SIDE, SIDE)
+        return x * SIDE + y, {"col_0": x, "col_1": y}
+
+    others = (10, 6, 14, 9, 11, 2, 8, 5, 7, 13, 15, 1, 3, 4, 12)
+    planes = (4, 3, 5, 2, 6, 1, 7)
 
     to_row = col // 2
     to_col = SPAN * lax.rem(col, 2) + z
@@ -69,6 +72,10 @@
 
     load_front = pltpu.make_async_copy(front, front_v, loc.at[0])
     load_front.start()
+    load_places = pltpu.make_async_copy(places_in, places, loc.at[5])
+    load_places.start()
+    load_dinv = pltpu.make_async_copy(dinv_in, dinv, loc.at[6])
+    load_dinv.start()
 
     barrier = pltpu.get_barrier_semaphore()
     for axis in ("col_0", "col_1"):
@@ -102,14 +109,16 @@
         arrive(slot(h, d0, d1), rg.at[h, d0, d1])
 
     for h in range(2):
-        for delta in (1, -1, 2):
+        for delta in (2, 1, -1):
             pass_on(h, 0, 0, 0, delta, mine(h))
-        for delta in (1, -1):
+    for h in range(2):
+        for delta in (2, 1, -1):
             pass_on(h, 0, 0, 1, delta, mine(h))
     keep = [pltpu.make_async_copy(mine(h), slot(h, 0, 0), loc.at[1 + h]) for h in range(2)]
     for copy in keep:
         copy.start()
 
+    load_places.wait()
     place = places[...]
 
     def chunk_of(bound):
@@ -128,51 +137,38 @@
     hit_rows = jnp.broadcast_to(jnp.max(mark, axis=1, keepdims=True), (own, LANES))
     hits[0] = hit_rows
 
-    for d in (1, 3):
+    for d in (1, 3, 2):
         for h in range(2):
             gathered(h, d, 0)
-            pass_on(h, d, 0, 1, 1)
-            pass_on(h, d, 0, 1, -1)
-    for h in range(2):
-        gathered(h, 0, 3)
-        pass_on(h, 0, 3, 1, 1)
-    for h in range(2):
-        gathered(h, 2, 0)
-        pass_on(h, 2, 0, 1, 1)
-        pass_on(h, 2, 0, 1, -1)
-    for h in range(2):
-        gathered(h, 1, 3)
-        pass_on(h, 1, 3, 1, 1)
-        gathered(h, 3, 1)
-        pass_on(h, 3, 1, 1, -1)
-    for h in range(2):
-        gathered(h, 2, 1)
-        pass_on(h, 2, 1, 1, -1)
+            for delta in (2, 1, -1):
+                pass_on(h, d, 0, 1, delta)
     for copy in keep:
         copy.wait()
     for h in range(2):
-        for d in ((0, 1), (2, 3), (3, 3), (1, 1), (0, 2), (1, 2), (2, 2), (3, 2)):
-            gathered(h, *d)
+        for d in range(SIDE):
+            for e in range(1, SIDE):
+                gathered(h, d, e)
 
     for h in range(2):
         for i in range(nwin):
-            wind[h, i, z] = gath[h, first + i]
-
-    def share(h, d):
-        return wind.at[h, :, lax.rem(z + d + SPAN, SPAN)]
+            wind[h, z, i] = gath[h, first + i]
+
+    cuts = ((0, nwin // 2), (nwin // 2, nwin - nwin // 2))
+
+    def share(h, u, d):
+        return wind.at[h, lax.rem(z + d + SPAN, SPAN), pl.ds(*cuts[u])]
 
     last = ((SPAN // 2, SPAN // 2 - 1), (SPAN // 2 - 1, SPAN // 2))
+    pieces = [(u, h, d, 1 - 2 * d) for u in range(2) for h in range(2) for d in range(2)]
     for s in range(1, SPAN // 2 + 1):
-        for h in range(2):
-            for d, sign in enumerate((1, -1)):
-                if s <= last[h][d]:
-                    if s > 1:
-                        arrive(share(h, -sign * (s - 1)), rz.at[h, d, s - 2])
-                    block = share(h, -sign * (s - 1))
-                    put(block, block, rz.at[h, d, s - 1], row=lax.rem(z + sign + SPAN, SPAN))
-    for h in range(2):
-        for d, sign in enumerate((1, -1)):
-            arrive(share(h, -sign * last[h][d]), rz.at[h, d, last[h][d] - 1])
+        for u, h, d, sign in pieces:
+            if s <= last[h][d]:
+                block = share(h, u, -sign * (s - 1))
+                if s > 1:
+                    arrive(block, rz.at[h, u, d, s - 2])
+                put(block, block, rz.at[h, u, d, s - 1], row=lax.rem(z + sign + SPAN, SPAN))
+    for u, h, d, sign in pieces:
+        arrive(share(h, u, -sign * last[h][d]), rz.at[h, u, d, last[h][d] - 1])
 
     rows_at = lax.broadcasted_iota(jnp.int32, (LANES, LANES), 0)
     for t in range(ntgt):
@@ -186,7 +182,9 @@
             axis=1,
         )
         for h in range(2):
-            rows = wind[h, pl.ds(a, 2)].reshape(2 * LANES, LANES)
+            rows = jnp.concatenate(
+                [wind[h, :, a + i].reshape(LANES, LANES) for i in range(2)], axis=0
+            )
             spread[pl.ds(t * LANES, LANES), pl.ds(h * LANES, LANES)] = jnp.dot(
                 table, rows, preferred_element_type=F32
             ).astype(BF16)
@@ -260,40 +258,25 @@
                 j = 2 * d + jj
                 post_1(part[h, 1 if d == 0 else 3, j] + fetch_1(h, d, SIDE + jj), h, d, j)
 
-    half = own // 2
-
-    def post_2(value, h, d, at):
-        post(value, out_2.at[h, d, at], ring_2.at[h, d, at], (1, h, d, at), r2,
-             step(order[h][1], 1 - 2 * d))
-
-    def fetch_2(h, d, at):
-        return fetch(ring_2.at[h, d, at], (1, h, d, at), r2)
-
     for j in (2, 1, 3, 0):
         for h in range(2):
             both = part[h, 0, j] + fetch_1(h, 0, j) + fetch_1(h, 1, j)
-            if j == 2:
-                for d in range(2):
-                    post_2(both[d * half:(d + 1) * half], h, d, 2)
+            if j:
+                post(both, out_2.at[h, j - 1], ring_2.at[h, j - 1], (1, h, 0, j - 1), r2,
+                     step(order[h][1], j))
             else:
-                mid[h, j // 2 if j else 2] = both
-            if j == 1:
-                post_2(both[half:], h, 0, 1)
-            if j == 3:
-                post_2(both[:half], h, 1, 0)
-    for h in range(2):
-        for d in range(2):
-            post_2(mid[h, d, pl.ds(d * half, half)] + fetch_2(h, d, 2), h, d, d)
+                mid[h] = both
     halves = []
     for h in range(2):
-        both = []
-        for u in range(2):
-            rows = mid[h, 2, pl.ds(u * half, half)]
-            both.append(rows + fetch_2(h, 0, u) + fetch_2(h, 1, u))
-        halves.append(jnp.concatenate(both, axis=0))
+        both = mid[h]
+        for j in (1, 3, 2):
+            both += fetch(ring_2.at[h, j - 1], (1, h, 0, j - 1), r2)
+        halves.append(both)
     hit_rows = hits[0]
     for h in range(2):
-        off_out[:, pl.ds(h * LANES, LANES)] = jnp.where(hit_rows > 0.5, -halves[h], 0.0)
+        off_v[:, pl.ds(h * LANES, LANES)] = jnp.where(hit_rows > 0.5, -halves[h], 0.0)
+    save_off = pltpu.make_async_copy(off_v, off_out, loc.at[7])
+    save_off.start()
     product = jnp.concatenate(halves, axis=1)
 
     @pl.when(goes)
@@ -307,17 +290,17 @@
     here = lax.dot_general(rows, high, dims, preferred_element_type=F32)
     here += lax.dot_general(rows, low, dims, preferred_element_type=F32)
     terms[...] = here.reshape(terms.shape)
-    for off in range(1, SIDE * SIDE):
+    for off in others:
         peer, device = in_plane(off)
         put(terms.at[peer], got_d.at[off - 1], rd.at[off - 1], **device)
     acc = terms[col]
-    for off in range(1, SIDE * SIDE):
+    for off in reversed(others):
         arrive(got_d.at[off - 1], rd.at[off - 1])
         acc += got_d[off - 1]
     sum_z[...] = acc
-    for off in range(1, SPAN):
+    for off in planes:
         put(sum_z, got_z.at[off - 1], rzz.at[off - 1], row=lax.rem(z + off, SPAN))
-    for off in range(1, SPAN):
+    for off in reversed(planes):
         arrive(got_z.at[off - 1], rzz.at[off - 1])
     acc = jnp.zeros_like(acc)
     got_z[SPAN - 1] = sum_z[...]
@@ -325,13 +308,19 @@
         at = lax.rem(z - r + SPAN - 1 + SPAN, SPAN)
         acc += got_z[at]
     total[col] = acc
-    for off in range(1, SIDE * SIDE):
+    for off in others:
         peer, device = in_plane(off)
         put(total.at[col], total.at[col], rt.at[off - 1], **device)
-    for off in range(1, SIDE * SIDE):
-        peer = lax.rem(col - off + SIDE * SIDE, SIDE * SIDE)
-        arrive(total.at[peer], rt.at[off - 1])
-    diag_out[...] = dinv[...] + total[...].reshape(dinv.shape)
+    for off in reversed(others):
+        x = lax.rem(px + SIDE - off // SIDE, SIDE)
+        y = lax.rem(py + SIDE - off % SIDE, SIDE)
+        arrive(total.at[x * SIDE + y], rt.at[off - 1])
+    load_dinv.wait()
+    diag_v[...] = dinv[...] + total[...].reshape(dinv.shape)
+    save_diag = pltpu.make_async_copy(diag_v, diag_out, loc.at[8])
+    save_diag.start()
+    save_off.wait()
+    save_diag.wait()
     for copy in sends:
         copy.wait_send()
 
@@ -360,25 +349,29 @@
         ),
         in_specs=[
             pl.BlockSpec(memory_space=pl.ANY),
-            pl.BlockSpec(memory_space=pltpu.VMEM),
-            pl.BlockSpec(memory_space=pl.ANY),
-            pl.BlockSpec(memory_space=pltpu.VMEM),
+            pl.BlockSpec(memory_space=pl.ANY),
+            pl.BlockSpec(memory_space=pl.ANY),
+            pl.BlockSpec(memory_space=pl.ANY),
         ],
         out_specs=(
-            pl.BlockSpec(memory_space=pltpu.VMEM),
-            pl.BlockSpec(memory_space=pltpu.VMEM),
+            pl.BlockSpec(memory_space=pl.ANY),
+            pl.BlockSpec(memory_space=pl.ANY),
         ),
         scratch_shapes=[
+            vmem((nchunk, LANES), jnp.int32),
+            vmem((width, width), F32),
+            vmem((own, width), F32),
+            vmem((width, width), F32),
             vmem((2, nchunk, GROUP, LANES), BF16),
-            vmem((2, nwin, SPAN, GROUP, LANES), BF16),
+            vmem((2, SPAN, nwin, GROUP, LANES), BF16),
             vmem((front_cols, width), BF16),
             vmem((front_rows, front_cols), BF16),
             vmem((2, SIDE, SIDE, own, LANES), F32),
             vmem((2, 2, SIDE + 2, own, LANES), jnp.int16),
             vmem((2, 2, SIDE + 2, own, LANES), jnp.int16),
-            vmem((2, 3, own, LANES), F32),
-            vmem((2, 2, 3, own // 2, LANES), jnp.int16),
-            vmem((2, 2, 3, own // 2, LANES), jnp.int16),
+            vmem((2, own, LANES), F32),
+            vmem((2, SIDE - 1, own, LANES), jnp.int16),
+            vmem((2, SIDE - 1, own, LANES), jnp.int16),
             vmem((2, 2, 2, 2, SIDE + 2, 1, LANES), F32),
             vmem((own, width), BF16),
             vmem((nown, own, LANES), F32),
@@ -389,14 +382,14 @@
             vmem((SIDE * SIDE, slab, width), F32),
             dma((160,)),
             dma((2, SIDE, SIDE)),
-            dma((2, 2, SPAN // 2)),
+            dma((2, 2, 2, SPAN // 2)),
             dma((2, 2, 2, SIDE + 2)),
-            dma((2, 2, 2, 3)),
+            dma((2, 2, 1, SIDE - 1)),
             dma,
             dma((SIDE * SIDE - 1,)),
             dma((SPAN - 1,)),
             dma((SIDE * SIDE - 1,)),
-            dma((5,)),
+            dma((9,)),
         ],
         compiler_params=pltpu.CompilerParams(
             collective_id=0, has_side_effects=True, vmem_limit_bytes=60 * 1024 * 1024

time: 80.9 us -> 74.2 us (0.917)
  Pallas kernels: 80.2 us -> 73.5 us
    pallas_call x1, Pallas kernels: 78.4 us -> 71.6 us  [shards(): pl.pallas_call(kernel, out_shape=(jax.ShapeDtypeStruct((own, width), F32)...]
where the time goes in v3:
time: 74.2 us; the launch traced here: 74.1 us
  Pallas kernels  73.5 us (99%)
    pallas_call x1, Pallas kernels, shards(): pl.pallas_call(kernel, out_shape=(jax.ShapeDtypeStruct((own, width), F32)...  71.6 us
    pallas_call x1, Pallas kernels, shards(): pl.pallas_call(finish, out_shape=(jax.ShapeDtypeStruct((own, width), F32)...  1.84 us

profile of v3, /device:TPU:32, one launch (start us, length us, event | category | flops | bytes accessed | tf_op | source)
XLA Modules:
  0.0 74.1 jit_solution(3194309391410746674)
XLA Ops:
  0.6 71.6 %selected_inverse.1 = (f32[192,256]{1,0:T(8,128)}, f32[256,256]{1,0:T(8,128)}) custom-call(bf16[6,8,16,256]{3,2,1,0:T(8,128)(2,1)} %bitcast.5, s32[96,128]{1,0:T(8,128)} %bitcast.7, bf16[3072,1536]{1,0:T(8,128)(2,1)} %front.1, f32[256,256]{1,0:T(8,128)} %bitcast.6), custom_call_target="tpu_custom_call" | custom-call | tf_op jit(solution)/shard_map/selected_inverse/pallas_call | solution.py:344
  72.3 1.8 %outputs.1 = (f32[192,256]{1,0:T(8,128)}, f32[256,256]{1,0:T(8,128)}) custom-call(f32[192,256]{1,0:T(8,128)} %get-tuple-element.6.off, f32[256,256]{1,0:T(8,128)} %get-tuple-element.7.diag), custom_call_target="tpu_custom_call" | custom-call | tf_op jit(solution)/shard_map/outputs/pallas_call | solution.py:405

commit v4 on v3

--- a/solution.py
+++ b/solution.py
@@ -23,7 +23,7 @@
 
 def kernel(
     panel, places_in, front, dinv_in, off_out, diag_out,
-    places, dinv, off_v, diag_v, gath, wind, spread, front_v, part, out_1, ring_1, mid, out_2, ring_2, scale, own_s, hits,
+    places, dinv, gath, wind, spread, front_v, part, out_1, ring_1, mid, out_2, ring_2, scale, own_s, hits,
     terms, got_d, sum_z, got_z, total,
     send, rg, rz, r1, r2, rs, rd, rzz, rt, loc,
 ):
@@ -38,18 +38,17 @@
     px, py = pos["col_0"], pos["col_1"]
     col = px * SIDE + py
     order = (("col_0", "col_1"), ("col_1", "col_0"))
-    sends = []
-
-    def put(src, dst, sem, **device):
-        copy = pltpu.make_async_remote_copy(
-            src_ref=src, dst_ref=dst, send_sem=send.at[len(sends)], recv_sem=sem,
+    def put(src, dst, out, sem, **device):
+        pltpu.make_async_remote_copy(
+            src_ref=src, dst_ref=dst, send_sem=send.at[out], recv_sem=sem,
             device_id=device, device_id_type=MESH_ID,
-        )
-        copy.start()
-        sends.append(copy)
+        ).start()
 
     def arrive(dst, sem):
         pltpu.make_async_copy(dst, dst, sem).wait()
+
+    def sent(same_bytes, out):
+        pltpu.make_async_copy(same_bytes, same_bytes, send.at[out]).wait()
 
     def step(axis, delta):
         return {axis: lax.rem(pos[axis] + delta + SIDE, SIDE)}
@@ -83,12 +82,12 @@
             pl.semaphore_signal(
                 barrier, inc=1, device_id=step(axis, delta), device_id_type=MESH_ID
             )
-    for delta in (1, -1):
+    for delta in (2, -2, 1, -1):
         pl.semaphore_signal(
             barrier, inc=1, device_id={"row": lax.rem(z + delta + SPAN, SPAN)},
             device_id_type=MESH_ID,
         )
-    pl.semaphore_wait(barrier, 2 * (SIDE - 1) + 2)
+    pl.semaphore_wait(barrier, 2 * (SIDE - 1) + 4)
 
     def slot(h, d0, d1):
         a0, a1 = order[h]
@@ -102,11 +101,11 @@
 
     def pass_on(h, d0, d1, which, delta, src=None):
         dst = slot(h, d0, d1)
-        d0, d1 = ((d0 - delta) % SIDE, d1) if which == 0 else (d0, (d1 - delta) % SIDE)
-        put(dst if src is None else src, dst, rg.at[h, d0, d1], **step(order[h][which], delta))
-
-    def gathered(h, d0, d1):
-        arrive(slot(h, d0, d1), rg.at[h, d0, d1])
+        sem = rg.at[h, 0 if which else (d0 - delta) % SIDE]
+        put(dst if src is None else src, dst, h, sem, **step(order[h][which], delta))
+
+    def gathered(h, d0):
+        arrive(slot(h, d0, 0), rg.at[h, d0])
 
     for h in range(2):
         for delta in (2, 1, -1):
@@ -139,15 +138,13 @@
 
     for d in (1, 3, 2):
         for h in range(2):
-            gathered(h, d, 0)
+            gathered(h, d)
             for delta in (2, 1, -1):
                 pass_on(h, d, 0, 1, delta)
     for copy in keep:
         copy.wait()
     for h in range(2):
-        for d in range(SIDE):
-            for e in range(1, SIDE):
-                gathered(h, d, e)
+        arrive(gath.at[h, pl.ds(0, SIDE * (SIDE - 1) * nblk)], rg.at[h, 0])
 
     for h in range(2):
         for i in range(nwin):
@@ -158,17 +155,47 @@
     def share(h, u, d):
         return wind.at[h, lax.rem(z + d + SPAN, SPAN), pl.ds(*cuts[u])]
 
-    last = ((SPAN // 2, SPAN // 2 - 1), (SPAN // 2 - 1, SPAN // 2))
     pieces = [(u, h, d, 1 - 2 * d) for u in range(2) for h in range(2) for d in range(2)]
-    for s in range(1, SPAN // 2 + 1):
-        for u, h, d, sign in pieces:
-            if s <= last[h][d]:
-                block = share(h, u, -sign * (s - 1))
-                if s > 1:
-                    arrive(block, rz.at[h, u, d, s - 2])
-                put(block, block, rz.at[h, u, d, s - 1], row=lax.rem(z + sign + SPAN, SPAN))
-    for u, h, d, sign in pieces:
-        arrive(share(h, u, -sign * last[h][d]), rz.at[h, u, d, last[h][d] - 1])
+
+    def pass_z(u, h, d, sign, origin, hops):
+        block = share(h, u, -sign * origin)
+        put(block, block, 2 + 2 * u + h, rz.at[h, u, d, origin + hops - 1],
+            row=lax.rem(z + sign * hops + SPAN, SPAN))
+
+    def came_z(u, h, d, sign, origin):
+        arrive(share(h, u, -sign * origin), rz.at[h, u, d, origin - 1])
+
+    for u, h, d, sign in pieces:
+        if h != d:
+            pass_z(u, h, d, sign, 0, 1)
+    for u, h, d, sign in pieces:
+        if h == d:
+            pass_z(u, h, d, sign, 0, 2)
+    for u, h, d, sign in pieces:
+        if h == d:
+            pass_z(u, h, d, sign, 0, 1)
+    for u, h, d, sign in pieces:
+        if h != d:
+            came_z(u, h, d, sign, 1)
+            pass_z(u, h, d, sign, 1, 1)
+    for u, h, d, sign in pieces:
+        if h == d:
+            came_z(u, h, d, sign, 2)
+            pass_z(u, h, d, sign, 2, 1)
+    for u, h, d, sign in pieces:
+        if h != d:
+            came_z(u, h, d, sign, 2)
+            pass_z(u, h, d, sign, 2, 1)
+    for u, h, d, sign in pieces:
+        if h == d:
+            came_z(u, h, d, sign, 3)
+            pass_z(u, h, d, sign, 3, 1)
+    for u, h, d, sign in pieces:
+        if h == d:
+            came_z(u, h, d, sign, 1)
+            came_z(u, h, d, sign, 4)
+        else:
+            came_z(u, h, d, sign, 3)
 
     rows_at = lax.broadcasted_iota(jnp.int32, (LANES, LANES), 0)
     for t in range(ntgt):
@@ -205,24 +232,25 @@
         copy.start()
         copy.wait()
 
-    def post(value, out, dst, at, sem, device):
+    def post(value, out, dst, at, sem, device, sems):
         top = jnp.maximum(jnp.max(jnp.abs(value), axis=0, keepdims=True), TINY)
         out[...] = jnp.round(value * (LEVELS / top)).astype(jnp.int32).astype(jnp.int16)
         scale[(0, *at)] = top * (1.0 / LEVELS)
-        put(scale.at[(0, *at)], scale.at[(1, *at)], sem.at[(1, *at[1:])], **device)
-        put(out, dst, sem.at[(0, *at[1:])], **device)
-
-    def fetch(dst, at, sem):
-        arrive(scale.at[(1, *at)], sem.at[(1, *at[1:])])
-        arrive(dst, sem.at[(0, *at[1:])])
+        put(scale.at[(0, *at)], scale.at[(1, *at)], sems[1], sem[1], **device)
+        put(out, dst, sems[0], sem[0], **device)
+
+    def value_of(dst, at):
         return dst[...].astype(jnp.int32).astype(F32) * scale[(1, *at)]
 
     def post_1(value, h, d, at):
-        post(value, out_1.at[h, d, at], ring_1.at[h, d, at], (0, h, d, at), r1,
-             step(order[h][0], 1 - 2 * d))
+        post(value, out_1.at[h, d, at], ring_1.at[h, d, at], (0, h, d, at),
+             (r1.at[0, h, d, at], r1.at[1, h, d, at]), step(order[h][0], 1 - 2 * d),
+             (6 + h, 8 + h))
 
     def fetch_1(h, d, at):
-        return fetch(ring_1.at[h, d, at], (0, h, d, at), r1)
+        arrive(scale.at[1, 0, h, d, at], r1.at[1, h, d, at])
+        arrive(ring_1.at[h, d, at], r1.at[0, h, d, at])
+        return value_of(ring_1.at[h, d, at], (0, h, d, at))
 
     def near(h, d, j):
         post_1(part[h, 1 if d == 0 else 3, j], h, d, j)
@@ -231,27 +259,33 @@
         post_1(part[h, 2, j], h, d, SIDE + j % 2)
 
     load_front.wait()
-    stripe = SIDE * own
-    for d in (2, 1, 3, 0):
-        at = pl.multiple_of(lax.rem(px + d, SIDE) * stripe, stripe)
-        block = jnp.dot(
-            front_v[pl.ds(at, stripe), :], spread[...], preferred_element_type=F32
-        )
-        for y in range(SIDE):
-            j = lax.rem(y - py + SIDE, SIDE)
-            part[0, d, j] = block[y * own:(y + 1) * own, :LANES]
-            part[1, j, d] = block[y * own:(y + 1) * own, LANES:]
-        if d == 2:
-            for j in range(SIDE):
-                far(0, j // 2, j)
-        if d == 1:
-            near(0, 0, 2)
-            near(0, 0, 3)
-        if d == 3:
-            near(0, 1, 0)
-            near(0, 1, 1)
-        far(1, d // 2, d)
-        near(1, 0 if d >= 2 else 1, d)
+
+    def rows_of(dx, dy):
+        at = (lax.rem(px + dx, SIDE) * SIDE + lax.rem(py + dy, SIDE)) * own
+        return front_v[pl.ds(pl.multiple_of(at, GROUP), own), :]
+
+    def multiply(*blocks):
+        rows = jnp.concatenate([rows_of(*block) for block in blocks], axis=0)
+        whole = jnp.dot(rows, spread[...], preferred_element_type=F32)
+        for n, (dx, dy) in enumerate(blocks):
+            part[0, dx, dy] = whole[n * own:(n + 1) * own, :LANES]
+            part[1, dy, dx] = whole[n * own:(n + 1) * own, LANES:]
+
+    multiply((2, 0), (2, 2), (2, 1), (2, 3))
+    for j in (0, 2, 1, 3):
+        far(0, j // 2, j)
+    far(1, 1, 2)
+    near(1, 0, 2)
+    multiply((0, 2), (1, 2), (3, 2))
+    for j in (0, 1, 3):
+        far(1, j // 2, j)
+    near(0, 0, 2)
+    multiply((1, 3), (3, 1), (3, 0), (0, 3))
+    for h in range(2):
+        near(h, 0, 3)
+        near(h, 1, 0)
+        near(h, 1, 1)
+    multiply((1, 0), (0, 1), (3, 3), (1, 1), (0, 0))
     for jj in range(2):
         for h in range(2):
             for d in range(2):
@@ -262,21 +296,21 @@
         for h in range(2):
             both = part[h, 0, j] + fetch_1(h, 0, j) + fetch_1(h, 1, j)
             if j:
-                post(both, out_2.at[h, j - 1], ring_2.at[h, j - 1], (1, h, 0, j - 1), r2,
-                     step(order[h][1], j))
+                post(both, out_2.at[h, j - 1], ring_2.at[h, j - 1], (1, h, 0, j - 1),
+                     (r2.at[0, h], r2.at[1, h]), step(order[h][1], j), (10 + h, 12 + h))
             else:
                 mid[h] = both
     halves = []
     for h in range(2):
+        arrive(scale.at[1, 1, h, 0, pl.ds(0, SIDE - 1)], r2.at[1, h])
+        arrive(ring_2.at[h], r2.at[0, h])
         both = mid[h]
         for j in (1, 3, 2):
-            both += fetch(ring_2.at[h, j - 1], (1, h, 0, j - 1), r2)
+            both += value_of(ring_2.at[h, j - 1], (1, h, 0, j - 1))
         halves.append(both)
     hit_rows = hits[0]
     for h in range(2):
-        off_v[:, pl.ds(h * LANES, LANES)] = jnp.where(hit_rows > 0.5, -halves[h], 0.0)
-    save_off = pltpu.make_async_copy(off_v, off_out, loc.at[7])
-    save_off.start()
+        off_out[:, pl.ds(h * LANES, LANES)] = jnp.where(hit_rows > 0.5, -halves[h], 0.0)
     product = jnp.concatenate(halves, axis=1)
 
     @pl.when(goes)
@@ -292,16 +326,15 @@
     terms[...] = here.reshape(terms.shape)
     for off in others:
         peer, device = in_plane(off)
-        put(terms.at[peer], got_d.at[off - 1], rd.at[off - 1], **device)
+        put(terms.at[peer], got_d.at[off - 1], 14, rd, **device)
     acc = terms[col]
-    for off in reversed(others):
-        arrive(got_d.at[off - 1], rd.at[off - 1])
+    arrive(got_d, rd)
+    for off in others:
         acc += got_d[off - 1]
     sum_z[...] = acc
     for off in planes:
-        put(sum_z, got_z.at[off - 1], rzz.at[off - 1], row=lax.rem(z + off, SPAN))
-    for off in reversed(planes):
-        arrive(got_z.at[off - 1], rzz.at[off - 1])
+        put(sum_z, got_z.at[off - 1], 15, rzz, row=lax.rem(z + off, SPAN))
+    arrive(got_z.at[pl.ds(0, SPAN - 1)], rzz)
     acc = jnp.zeros_like(acc)
     got_z[SPAN - 1] = sum_z[...]
     for r in range(SPAN):
@@ -310,24 +343,32 @@
     total[col] = acc
     for off in others:
         peer, device = in_plane(off)
-        put(total.at[col], total.at[col], rt.at[off - 1], **device)
-    for off in reversed(others):
-        x = lax.rem(px + SIDE - off // SIDE, SIDE)
-        y = lax.rem(py + SIDE - off % SIDE, SIDE)
-        arrive(total.at[x * SIDE + y], rt.at[off - 1])
+        put(total.at[col], total.at[col], 16, rt, **device)
+    arrive(total.at[pl.ds(0, SIDE * SIDE - 1)], rt)
     load_dinv.wait()
-    diag_v[...] = dinv[...] + total[...].reshape(dinv.shape)
-    save_diag = pltpu.make_async_copy(diag_v, diag_out, loc.at[8])
-    save_diag.start()
-    save_off.wait()
-    save_diag.wait()
-    for copy in sends:
-        copy.wait_send()
-
-
-def finish(off, diag, off_out, diag_out):
-    off_out[...] = off[...]
-    diag_out[...] = diag[...]
+    diag_out[...] = dinv[...] + total[...].reshape(dinv.shape)
+    for h in range(2):
+        sent(gath.at[h, pl.ds(0, (SIDE * SIDE - 1) * nblk)], h)
+        for u in range(2):
+            sent(gath.at[h, pl.ds(0, (SPAN - 1) * cuts[u][1])], 2 + 2 * u + h)
+        sent(out_1.at[h], 6 + h)
+        sent(scale.at[0, 0, h], 8 + h)
+        sent(out_2.at[h], 10 + h)
+        sent(scale.at[0, 1, h, 0, pl.ds(0, SIDE - 1)], 12 + h)
+    sent(got_d, 14)
+    sent(got_z.at[pl.ds(0, SPAN - 1)], 15)
+    sent(total.at[pl.ds(0, SIDE * SIDE - 1)], 16)
+
+
+def finish(off, diag, off_out, diag_out, sems):
+    copies = [
+        pltpu.make_async_copy(off, off_out, sems.at[0]),
+        pltpu.make_async_copy(diag, diag_out, sems.at[1]),
+    ]
+    for copy in copies:
+        copy.start()
+    for copy in copies:
+        copy.wait()
 
 
 def shards(front_inverse, panel, row_map, diag_inverse):
@@ -347,20 +388,10 @@
             jax.ShapeDtypeStruct((own, width), F32),
             jax.ShapeDtypeStruct((width, width), F32),
         ),
-        in_specs=[
-            pl.BlockSpec(memory_space=pl.ANY),
-            pl.BlockSpec(memory_space=pl.ANY),
-            pl.BlockSpec(memory_space=pl.ANY),
-            pl.BlockSpec(memory_space=pl.ANY),
-        ],
-        out_specs=(
-            pl.BlockSpec(memory_space=pl.ANY),
-            pl.BlockSpec(memory_space=pl.ANY),
-        ),
+        in_specs=[pl.BlockSpec(memory_space=pltpu.HBM)] * 4,
+        out_specs=(pl.BlockSpec(memory_space=pltpu.VMEM),) * 2,
         scratch_shapes=[
             vmem((nchunk, LANES), jnp.int32),
-            vmem((width, width), F32),
-            vmem((own, width), F32),
             vmem((width, width), F32),
             vmem((2, nchunk, GROUP, LANES), BF16),
             vmem((2, SPAN, nwin, GROUP, LANES), BF16),
@@ -380,28 +411,33 @@
             vmem((slab, width), F32),
             vmem((SPAN, slab, width), F32),
             vmem((SIDE * SIDE, slab, width), F32),
-            dma((160,)),
-            dma((2, SIDE, SIDE)),
+            dma((17,)),
+            dma((2, SIDE)),
             dma((2, 2, 2, SPAN // 2)),
             dma((2, 2, 2, SIDE + 2)),
-            dma((2, 2, 1, SIDE - 1)),
+            dma((2, 2)),
             dma,
-            dma((SIDE * SIDE - 1,)),
-            dma((SPAN - 1,)),
-            dma((SIDE * SIDE - 1,)),
-            dma((9,)),
+            dma,
+            dma,
+            dma,
+            dma((7,)),
         ],
         compiler_params=pltpu.CompilerParams(
-            collective_id=0, has_side_effects=True, vmem_limit_bytes=60 * 1024 * 1024
+            collective_id=0, has_side_effects=True, vmem_limit_bytes=32 * 1024 * 1024
         ),
         name="selected_inverse",
     )(
-        panel.reshape(block // (SPAN * GROUP), SPAN, GROUP, width),
-        row_map.reshape(nchunk, LANES),
-        front_inverse,
-        diag_inverse[0],
+        *(
+            pltpu.with_memory_space_constraint(x, pltpu.HBM)
+            for x in (
+                panel.reshape(block // (SPAN * GROUP), SPAN, GROUP, width),
+                row_map.reshape(nchunk, LANES),
+                front_inverse,
+                diag_inverse[0],
+            )
+        )
     )
-    whole = pl.BlockSpec(memory_space=pltpu.VMEM)
+    whole = pl.BlockSpec(memory_space=pl.ANY)
     offdiag, diag = pl.pallas_call(
         finish,
         out_shape=(
@@ -410,8 +446,9 @@
         ),
         in_specs=[whole, whole],
         out_specs=(whole, whole),
+        scratch_shapes=[dma((2,))],
         name="outputs",
-    )(offdiag, diag)
+    )(*(pltpu.with_memory_space_constraint(x, pltpu.VMEM) for x in (offdiag, diag)))
     return offdiag[None], diag[None]
 
 

time: 74.2 us -> 67 us (0.903)
  Pallas kernels: 73.5 us -> 66.3 us
    pallas_call x1, Pallas kernels: 71.6 us -> 65.5 us  [shards(): pl.pallas_call(kernel, out_shape=(jax.ShapeDtypeStruct((own, width), F32)...]
    pallas_call x1, Pallas kernels: 1.84 us -> 0.79 us  [shards(): pl.pallas_call(finish, out_shape=(jax.ShapeDtypeStruct((own, width), F32)...]
where the time goes in v4:
time: 67 us
  Pallas kernels  66.3 us (99%)
    pallas_call x1, Pallas kernels, shards(): pl.pallas_call(kernel, out_shape=(jax.ShapeDtypeStruct((own, width), F32)...  65.5 us

profile of v4, /device:TPU:32, one launch (start us, length us, event | category | flops | bytes accessed | tf_op | source)
XLA Modules:
  0.0 67.0 jit_solution(9375223018832481292)
XLA Ops:
  0.6 65.5 %selected_inverse.1 = (f32[192,256]{1,0:T(8,128)S(1)}, f32[256,256]{1,0:T(8,128)S(1)}) custom-call(bf16[6,8,16,256]{3,2,1,0:T(8,128)(2,1)} %bitcast.5, s32[96,128]{1,0:T(8,128)} %bitcast.7, bf16[3072,1536]{1,0:T(8,128)(2,1)} %front.1, f32[256,256]{1,0:T(8,128)} %bitcast.6), custom_call_target="tpu_custom_call" | custom-call | tf_op jit(solution)/shard_map/selected_inverse/pallas_call | solution.py:385
  66.2 0.8 %outputs.1 = (f32[192,256]{1,0:T(8,128)}, f32[256,256]{1,0:T(8,128)}) custom-call(f32[192,256]{1,0:T(8,128)S(1)} %get-tuple-element.6.off, f32[256,256]{1,0:T(8,128)S(1)} %get-tuple-element.7.diag), custom_call_target="tpu_custom_call" | custom-call | tf_op jit(solution)/shard_map/outputs/pallas_call | solution.py:441

commit v5 on v4

--- a/solution.py
+++ b/solution.py
@@ -24,7 +24,7 @@
 def kernel(
     panel, places_in, front, dinv_in, off_out, diag_out,
     places, dinv, gath, wind, spread, front_v, part, out_1, ring_1, mid, out_2, ring_2, scale, own_s, hits,
-    terms, got_d, sum_z, got_z, total,
+    terms, got_d, got_z, total, dscale,
     send, rg, rz, r1, r2, rs, rd, rzz, rt, loc,
 ):
     nblk = panel.shape[0]
@@ -271,26 +271,29 @@
             part[0, dx, dy] = whole[n * own:(n + 1) * own, :LANES]
             part[1, dy, dx] = whole[n * own:(n + 1) * own, LANES:]
 
-    multiply((2, 0), (2, 2), (2, 1), (2, 3))
-    for j in (0, 2, 1, 3):
-        far(0, j // 2, j)
-    far(1, 1, 2)
-    near(1, 0, 2)
-    multiply((0, 2), (1, 2), (3, 2))
-    for j in (0, 1, 3):
-        far(1, j // 2, j)
-    near(0, 0, 2)
-    multiply((1, 3), (3, 1), (3, 0), (0, 3))
-    for h in range(2):
+    multiply((2, 2))
+    for h in range(2):
+        far(h, 1, 2)
+    multiply((2, 1), (1, 2), (2, 3), (3, 2))
+    for j in (1, 3):
+        for h in range(2):
+            far(h, j // 2, j)
+    for h in range(2):
+        near(h, 0, 2)
+    multiply((2, 0), (0, 2), (1, 3), (3, 1))
+    for h in range(2):
+        far(h, 0, 0)
+    for h in range(2):
+        near(h, 1, 1)
         near(h, 0, 3)
+    multiply((3, 0), (0, 3))
+    for h in range(2):
         near(h, 1, 0)
-        near(h, 1, 1)
-    multiply((1, 0), (0, 1), (3, 3), (1, 1), (0, 0))
-    for jj in range(2):
+    multiply((3, 3), (1, 1), (1, 0), (0, 1), (0, 0))
+    for j in (2, 1, 3, 0):
         for h in range(2):
-            for d in range(2):
-                j = 2 * d + jj
-                post_1(part[h, 1 if d == 0 else 3, j] + fetch_1(h, d, SIDE + jj), h, d, j)
+            d = j // 2
+            post_1(part[h, 1 if d == 0 else 3, j] + fetch_1(h, d, SIDE + j % 2), h, d, j)
 
     for j in (2, 1, 3, 0):
         for h in range(2):
@@ -323,30 +326,46 @@
     dims = (((0,), (0,)), ((), ()))
     here = lax.dot_general(rows, high, dims, preferred_element_type=F32)
     here += lax.dot_general(rows, low, dims, preferred_element_type=F32)
-    terms[...] = here.reshape(terms.shape)
+
+    def code(value):
+        top = jnp.maximum(jnp.max(jnp.abs(value), axis=-2, keepdims=True), TINY)
+        levels = jnp.round(value * (LEVELS / top)).astype(jnp.int32).astype(jnp.int16)
+        return levels, top * (1.0 / LEVELS)
+
+    def plain(levels, unit):
+        return levels.astype(jnp.int32).astype(F32) * unit
+
+    here = here.reshape(terms.shape)
+    terms[...], dscale[0] = code(here)
     for off in others:
         peer, device = in_plane(off)
-        put(terms.at[peer], got_d.at[off - 1], 14, rd, **device)
-    acc = terms[col]
-    arrive(got_d, rd)
+        put(dscale.at[0, peer], dscale.at[1, off - 1], 17, rd.at[1], **device)
+        put(terms.at[peer], got_d.at[off - 1], 14, rd.at[0], **device)
+    acc = plain(terms[col], dscale[0, col])
+    arrive(dscale.at[1, pl.ds(0, SIDE * SIDE - 1)], rd.at[1])
+    arrive(got_d, rd.at[0])
     for off in others:
-        acc += got_d[off - 1]
-    sum_z[...] = acc
+        acc += plain(got_d[off - 1], dscale[1, off - 1])
+    got_z[SPAN - 1], dscale[2, SPAN - 1] = code(acc)
     for off in planes:
-        put(sum_z, got_z.at[off - 1], 15, rzz, row=lax.rem(z + off, SPAN))
-    arrive(got_z.at[pl.ds(0, SPAN - 1)], rzz)
+        peer = lax.rem(z + off, SPAN)
+        put(dscale.at[2, SPAN - 1], dscale.at[2, off - 1], 18, rzz.at[1], row=peer)
+        put(got_z.at[SPAN - 1], got_z.at[off - 1], 15, rzz.at[0], row=peer)
+    arrive(dscale.at[2, pl.ds(0, SPAN - 1)], rzz.at[1])
+    arrive(got_z.at[pl.ds(0, SPAN - 1)], rzz.at[0])
     acc = jnp.zeros_like(acc)
-    got_z[SPAN - 1] = sum_z[...]
     for r in range(SPAN):
         at = lax.rem(z - r + SPAN - 1 + SPAN, SPAN)
-        acc += got_z[at]
-    total[col] = acc
+        acc += plain(got_z[at], dscale[2, at])
+    total[col], dscale[3, col] = code(acc)
     for off in others:
         peer, device = in_plane(off)
-        put(total.at[col], total.at[col], 16, rt, **device)
-    arrive(total.at[pl.ds(0, SIDE * SIDE - 1)], rt)
+        put(dscale.at[3, col], dscale.at[3, col], 19, rt.at[1], **device)
+        put(total.at[col], total.at[col], 16, rt.at[0], **device)
+    arrive(dscale.at[3, pl.ds(0, SIDE * SIDE - 1)], rt.at[1])
+    arrive(total.at[pl.ds(0, SIDE * SIDE - 1)], rt.at[0])
     load_dinv.wait()
-    diag_out[...] = dinv[...] + total[...].reshape(dinv.shape)
+    diag_out[...] = dinv[...] + plain(total[...], dscale[3]).reshape(dinv.shape)
     for h in range(2):
         sent(gath.at[h, pl.ds(0, (SIDE * SIDE - 1) * nblk)], h)
         for u in range(2):
@@ -357,6 +376,9 @@
         sent(scale.at[0, 1, h, 0, pl.ds(0, SIDE - 1)], 12 + h)
     sent(got_d, 14)
     sent(got_z.at[pl.ds(0, SPAN - 1)], 15)
+    for at in (17, 19):
+        sent(dscale.at[1, pl.ds(0, SIDE * SIDE - 1)], at)
+    sent(dscale.at[2, pl.ds(0, SPAN - 1)], 18)
     sent(total.at[pl.ds(0, SIDE * SIDE - 1)], 16)
 
 
@@ -406,20 +428,20 @@
             vmem((2, 2, 2, 2, SIDE + 2, 1, LANES), F32),
             vmem((own, width), BF16),
             vmem((nown, own, LANES), F32),
-            vmem((SIDE * SIDE, slab, width), F32),
-            vmem((SIDE * SIDE - 1, slab, width), F32),
-            vmem((slab, width), F32),
-            vmem((SPAN, slab, width), F32),
-            vmem((SIDE * SIDE, slab, width), F32),
-            dma((17,)),
+            vmem((SIDE * SIDE, slab, width), jnp.int16),
+            vmem((SIDE * SIDE - 1, slab, width), jnp.int16),
+            vmem((SPAN, slab, width), jnp.int16),
+            vmem((SIDE * SIDE, slab, width), jnp.int16),
+            vmem((4, SIDE * SIDE, 1, width), F32),
+            dma((20,)),
             dma((2, SIDE)),
             dma((2, 2, 2, SPAN // 2)),
             dma((2, 2, 2, SIDE + 2)),
             dma((2, 2)),
             dma,
-            dma,
-            dma,
-            dma,
+            dma((2,)),
+            dma((2,)),
+            dma((2,)),
             dma((7,)),
         ],
         compiler_params=pltpu.CompilerParams(

time: 67 us -> 65 us (0.970)
  Pallas kernels: 66.3 us -> 64.3 us
    pallas_call x1, Pallas kernels: 65.5 us -> 63.5 us  [shards(): pl.pallas_call(kernel, out_shape=(jax.ShapeDtypeStruct((own, width), F32)...]
where the time goes in v5:
time: 65 us
  Pallas kernels  64.3 us (99%)
    pallas_call x1, Pallas kernels, shards(): pl.pallas_call(kernel, out_shape=(jax.ShapeDtypeStruct((own, width), F32)...  63.5 us

profile of v5, /device:TPU:32, one launch (start us, length us, event | category | flops | bytes accessed | tf_op | source)
XLA Modules:
  0.0 65.0 jit_solution(4315678549125461294)
XLA Ops:
  0.6 63.5 %selected_inverse.1 = (f32[192,256]{1,0:T(8,128)S(1)}, f32[256,256]{1,0:T(8,128)S(1)}) custom-call(bf16[6,8,16,256]{3,2,1,0:T(8,128)(2,1)} %bitcast.5, s32[96,128]{1,0:T(8,128)} %bitcast.7, bf16[3072,1536]{1,0:T(8,128)(2,1)} %front.1, f32[256,256]{1,0:T(8,128)} %bitcast.6), custom_call_target="tpu_custom_call" | custom-call | tf_op jit(solution)/shard_map/selected_inverse/pallas_call | solution.py:407
  64.2 0.8 %outputs.1 = (f32[192,256]{1,0:T(8,128)}, f32[256,256]{1,0:T(8,128)}) custom-call(f32[192,256]{1,0:T(8,128)S(1)} %get-tuple-element.6.off, f32[256,256]{1,0:T(8,128)S(1)} %get-tuple-element.7.diag), custom_call_target="tpu_custom_call" | custom-call | tf_op jit(solution)/shard_map/outputs/pallas_call | solution.py:463

commit v6 on v5

--- a/solution.py
+++ b/solution.py
@@ -102,7 +102,7 @@
     def pass_on(h, d0, d1, which, delta, src=None):
         dst = slot(h, d0, d1)
         sem = rg.at[h, 0 if which else (d0 - delta) % SIDE]
-        put(dst if src is None else src, dst, h, sem, **step(order[h][which], delta))
+        put(dst if src is None else src, dst, 0, sem, **step(order[h][which], delta))
 
     def gathered(h, d0):
         arrive(slot(h, d0, 0), rg.at[h, d0])
@@ -159,7 +159,7 @@
 
     def pass_z(u, h, d, sign, origin, hops):
         block = share(h, u, -sign * origin)
-        put(block, block, 2 + 2 * u + h, rz.at[h, u, d, origin + hops - 1],
+        put(block, block, 1 + u, rz.at[h, u, d, origin + hops - 1],
             row=lax.rem(z + sign * hops + SPAN, SPAN))
 
     def came_z(u, h, d, sign, origin):
@@ -181,6 +181,9 @@
     for u, h, d, sign in pieces:
         if h == d:
             came_z(u, h, d, sign, 2)
+            pass_z(u, h, d, sign, 2, 2)
+    for u, h, d, sign in pieces:
+        if h == d:
             pass_z(u, h, d, sign, 2, 1)
     for u, h, d, sign in pieces:
         if h != d:
@@ -188,11 +191,8 @@
             pass_z(u, h, d, sign, 2, 1)
     for u, h, d, sign in pieces:
         if h == d:
+            came_z(u, h, d, sign, 1)
             came_z(u, h, d, sign, 3)
-            pass_z(u, h, d, sign, 3, 1)
-    for u, h, d, sign in pieces:
-        if h == d:
-            came_z(u, h, d, sign, 1)
             came_z(u, h, d, sign, 4)
         else:
             came_z(u, h, d, sign, 3)
@@ -242,21 +242,26 @@
     def value_of(dst, at):
         return dst[...].astype(jnp.int32).astype(F32) * scale[(1, *at)]
 
-    def post_1(value, h, d, at):
+    def post_1(value, h, d, at, sem):
         post(value, out_1.at[h, d, at], ring_1.at[h, d, at], (0, h, d, at),
-             (r1.at[0, h, d, at], r1.at[1, h, d, at]), step(order[h][0], 1 - 2 * d),
-             (6 + h, 8 + h))
-
-    def fetch_1(h, d, at):
-        arrive(scale.at[1, 0, h, d, at], r1.at[1, h, d, at])
-        arrive(ring_1.at[h, d, at], r1.at[0, h, d, at])
+             (r1.at[0, h, sem], r1.at[1, h, sem]), step(order[h][0], 1 - 2 * d), (3, 4))
+
+    def fetch_far(h, j):
+        d, at = j // 2, SIDE + j % 2
+        arrive(scale.at[1, 0, h, d, at], r1.at[1, h, SIDE + j])
+        arrive(ring_1.at[h, d, at], r1.at[0, h, SIDE + j])
         return value_of(ring_1.at[h, d, at], (0, h, d, at))
 
+    def fetch_near(h, j):
+        arrive(scale.at[1, 0, h, :, j], r1.at[1, h, j])
+        arrive(ring_1.at[h, :, j], r1.at[0, h, j])
+        return [value_of(ring_1.at[h, d, j], (0, h, d, j)) for d in range(2)]
+
     def near(h, d, j):
-        post_1(part[h, 1 if d == 0 else 3, j], h, d, j)
+        post_1(part[h, 1 if d == 0 else 3, j], h, d, j, j)
 
     def far(h, d, j):
-        post_1(part[h, 2, j], h, d, SIDE + j % 2)
+        post_1(part[h, 2, j], h, d, SIDE + j % 2, SIDE + j)
 
     load_front.wait()
 
@@ -293,14 +298,15 @@
     for j in (2, 1, 3, 0):
         for h in range(2):
             d = j // 2
-            post_1(part[h, 1 if d == 0 else 3, j] + fetch_1(h, d, SIDE + j % 2), h, d, j)
+            post_1(part[h, 1 if d == 0 else 3, j] + fetch_far(h, j), h, d, j, j)
 
     for j in (2, 1, 3, 0):
         for h in range(2):
-            both = part[h, 0, j] + fetch_1(h, 0, j) + fetch_1(h, 1, j)
+            ahead, behind = fetch_near(h, j)
+            both = part[h, 0, j] + ahead + behind
             if j:
                 post(both, out_2.at[h, j - 1], ring_2.at[h, j - 1], (1, h, 0, j - 1),
-                     (r2.at[0, h], r2.at[1, h]), step(order[h][1], j), (10 + h, 12 + h))
+                     (r2.at[0, h], r2.at[1, h]), step(order[h][1], j), (5, 6))
             else:
                 mid[h] = both
     halves = []
@@ -339,8 +345,8 @@
     terms[...], dscale[0] = code(here)
     for off in others:
         peer, device = in_plane(off)
-        put(dscale.at[0, peer], dscale.at[1, off - 1], 17, rd.at[1], **device)
-        put(terms.at[peer], got_d.at[off - 1], 14, rd.at[0], **device)
+        put(dscale.at[0, peer], dscale.at[1, off - 1], 8, rd.at[1], **device)
+        put(terms.at[peer], got_d.at[off - 1], 7, rd.at[0], **device)
     acc = plain(terms[col], dscale[0, col])
     arrive(dscale.at[1, pl.ds(0, SIDE * SIDE - 1)], rd.at[1])
     arrive(got_d, rd.at[0])
@@ -349,8 +355,8 @@
     got_z[SPAN - 1], dscale[2, SPAN - 1] = code(acc)
     for off in planes:
         peer = lax.rem(z + off, SPAN)
-        put(dscale.at[2, SPAN - 1], dscale.at[2, off - 1], 18, rzz.at[1], row=peer)
-        put(got_z.at[SPAN - 1], got_z.at[off - 1], 15, rzz.at[0], row=peer)
+        put(dscale.at[2, SPAN - 1], dscale.at[2, off - 1], 10, rzz.at[1], row=peer)
+        put(got_z.at[SPAN - 1], got_z.at[off - 1], 9, rzz.at[0], row=peer)
     arrive(dscale.at[2, pl.ds(0, SPAN - 1)], rzz.at[1])
     arrive(got_z.at[pl.ds(0, SPAN - 1)], rzz.at[0])
     acc = jnp.zeros_like(acc)
@@ -360,26 +366,25 @@
     total[col], dscale[3, col] = code(acc)
     for off in others:
         peer, device = in_plane(off)
-        put(dscale.at[3, col], dscale.at[3, col], 19, rt.at[1], **device)
-        put(total.at[col], total.at[col], 16, rt.at[0], **device)
+        put(dscale.at[3, col], dscale.at[3, col], 12, rt.at[1], **device)
+        put(total.at[col], total.at[col], 11, rt.at[0], **device)
     arrive(dscale.at[3, pl.ds(0, SIDE * SIDE - 1)], rt.at[1])
     arrive(total.at[pl.ds(0, SIDE * SIDE - 1)], rt.at[0])
     load_dinv.wait()
     diag_out[...] = dinv[...] + plain(total[...], dscale[3]).reshape(dinv.shape)
-    for h in range(2):
-        sent(gath.at[h, pl.ds(0, (SIDE * SIDE - 1) * nblk)], h)
-        for u in range(2):
-            sent(gath.at[h, pl.ds(0, (SPAN - 1) * cuts[u][1])], 2 + 2 * u + h)
-        sent(out_1.at[h], 6 + h)
-        sent(scale.at[0, 0, h], 8 + h)
-        sent(out_2.at[h], 10 + h)
-        sent(scale.at[0, 1, h, 0, pl.ds(0, SIDE - 1)], 12 + h)
-    sent(got_d, 14)
-    sent(got_z.at[pl.ds(0, SPAN - 1)], 15)
-    for at in (17, 19):
-        sent(dscale.at[1, pl.ds(0, SIDE * SIDE - 1)], at)
-    sent(dscale.at[2, pl.ds(0, SPAN - 1)], 18)
-    sent(total.at[pl.ds(0, SIDE * SIDE - 1)], 16)
+    sent(gath.at[:, pl.ds(0, (SIDE * SIDE - 1) * nblk)], 0)
+    for u in range(2):
+        sent(gath.at[:, pl.ds(0, (SPAN - 1) * cuts[u][1])], 1 + u)
+    sent(out_1, 3)
+    sent(scale.at[0, 0], 4)
+    sent(out_2, 5)
+    sent(scale.at[0, 1, :, 0, pl.ds(0, SIDE - 1)], 6)
+    sent(got_d, 7)
+    sent(dscale.at[1, pl.ds(0, SIDE * SIDE - 1)], 8)
+    sent(got_z.at[pl.ds(0, SPAN - 1)], 9)
+    sent(dscale.at[2, pl.ds(0, SPAN - 1)], 10)
+    sent(dscale.at[3, pl.ds(0, SIDE * SIDE - 1)], 12)
+    sent(total.at[pl.ds(0, SIDE * SIDE - 1)], 11)
 
 
 def finish(off, diag, off_out, diag_out, sems):
@@ -433,10 +438,10 @@
             vmem((SPAN, slab, width), jnp.int16),
             vmem((SIDE * SIDE, slab, width), jnp.int16),
             vmem((4, SIDE * SIDE, 1, width), F32),
-            dma((20,)),
+            dma((13,)),
             dma((2, SIDE)),
             dma((2, 2, 2, SPAN // 2)),
-            dma((2, 2, 2, SIDE + 2)),
+            dma((2, 2, 2 * SIDE)),
             dma((2, 2)),
             dma,
             dma((2,)),

time: 65 us -> 64.6 us (level)
  no operation moved by 1% of the time
where the time goes in v6:
time: 64.6 us; the launch traced here: 64.5 us
  Pallas kernels  63.9 us (99%)
    pallas_call x1, Pallas kernels, shards(): pl.pallas_call(kernel, out_shape=(jax.ShapeDtypeStruct((own, width), F32)...  63.1 us

profile of v6, /device:TPU:32, one launch (start us, length us, event | category | flops | bytes accessed | tf_op | source)
XLA Modules:
  0.0 64.5 jit_solution(14505724475625818275)
XLA Ops:
  0.6 63.1 %selected_inverse.1 = (f32[192,256]{1,0:T(8,128)S(1)}, f32[256,256]{1,0:T(8,128)S(1)}) custom-call(bf16[6,8,16,256]{3,2,1,0:T(8,128)(2,1)} %bitcast.5, s32[96,128]{1,0:T(8,128)} %bitcast.7, bf16[3072,1536]{1,0:T(8,128)(2,1)} %front.1, f32[256,256]{1,0:T(8,128)} %bitcast.6), custom_call_target="tpu_custom_call" | custom-call | tf_op jit(solution)/shard_map/selected_inverse/pallas_call | solution.py:412
  63.7 0.8 %outputs.1 = (f32[192,256]{1,0:T(8,128)}, f32[256,256]{1,0:T(8,128)}) custom-call(f32[192,256]{1,0:T(8,128)S(1)} %get-tuple-element.6.off, f32[256,256]{1,0:T(8,128)S(1)} %get-tuple-element.7.diag), custom_call_target="tpu_custom_call" | custom-call | tf_op jit(solution)/shard_map/outputs/pallas_call | solution.py:468

commit v7 on v6

--- a/solution.py
+++ b/solution.py
@@ -69,16 +69,9 @@
     to_dev = {"row": to_row, "col_0": to_col // SIDE, "col_1": lax.rem(to_col, SIDE)}
     from_dev = {"row": from_row, "col_0": from_col // SIDE, "col_1": lax.rem(from_col, SIDE)}
 
-    load_front = pltpu.make_async_copy(front, front_v, loc.at[0])
-    load_front.start()
-    load_places = pltpu.make_async_copy(places_in, places, loc.at[5])
-    load_places.start()
-    load_dinv = pltpu.make_async_copy(dinv_in, dinv, loc.at[6])
-    load_dinv.start()
-
     barrier = pltpu.get_barrier_semaphore()
     for axis in ("col_0", "col_1"):
-        for delta in (1, -1, 2):
+        for delta in (2, 1, -1):
             pl.semaphore_signal(
                 barrier, inc=1, device_id=step(axis, delta), device_id_type=MESH_ID
             )
@@ -87,6 +80,12 @@
             barrier, inc=1, device_id={"row": lax.rem(z + delta + SPAN, SPAN)},
             device_id_type=MESH_ID,
         )
+    load_front = pltpu.make_async_copy(front, front_v, loc.at[0])
+    load_front.start()
+    load_places = pltpu.make_async_copy(places_in, places, loc.at[5])
+    load_places.start()
+    load_dinv = pltpu.make_async_copy(dinv_in, dinv, loc.at[6])
+    load_dinv.start()
     pl.semaphore_wait(barrier, 2 * (SIDE - 1) + 4)
 
     def slot(h, d0, d1):
@@ -172,12 +171,12 @@
         if h == d:
             pass_z(u, h, d, sign, 0, 2)
     for u, h, d, sign in pieces:
-        if h == d:
-            pass_z(u, h, d, sign, 0, 1)
-    for u, h, d, sign in pieces:
         if h != d:
             came_z(u, h, d, sign, 1)
             pass_z(u, h, d, sign, 1, 1)
+    for u, h, d, sign in pieces:
+        if h == d:
+            pass_z(u, h, d, sign, 0, 1)
     for u, h, d, sign in pieces:
         if h == d:
             came_z(u, h, d, sign, 2)

time: 64.6 us -> 64.4 us (level)
  no operation moved by 1% of the time
where the time goes in v7:
time: 64.4 us
  Pallas kernels  63.7 us (99%)
    pallas_call x1, Pallas kernels, shards(): pl.pallas_call(kernel, out_shape=(jax.ShapeDtypeStruct((own, width), F32)...  62.9 us

profile of v7, /device:TPU:32, one launch (start us, length us, event | category | flops | bytes accessed | tf_op | source)
XLA Modules:
  0.0 64.4 jit_solution(9226614985873105816)
XLA Ops:
  0.6 62.9 %selected_inverse.1 = (f32[192,256]{1,0:T(8,128)S(1)}, f32[256,256]{1,0:T(8,128)S(1)}) custom-call(bf16[6,8,16,256]{3,2,1,0:T(8,128)(2,1)} %bitcast.5, s32[96,128]{1,0:T(8,128)} %bitcast.7, bf16[3072,1536]{1,0:T(8,128)(2,1)} %front.1, f32[256,256]{1,0:T(8,128)} %bitcast.6), custom_call_target="tpu_custom_call" | custom-call | tf_op jit(solution)/shard_map/selected_inverse/pallas_call | solution.py:411
  63.6 0.8 %outputs.1 = (f32[192,256]{1,0:T(8,128)}, f32[256,256]{1,0:T(8,128)}) custom-call(f32[192,256]{1,0:T(8,128)S(1)} %get-tuple-element.6.off, f32[256,256]{1,0:T(8,128)S(1)} %get-tuple-element.7.diag), custom_call_target="tpu_custom_call" | custom-call | tf_op jit(solution)/shard_map/outputs/pallas_call | solution.py:467

commit v8 on v6

--- a/solution.py
+++ b/solution.py
@@ -279,10 +279,12 @@
     multiply((2, 2))
     for h in range(2):
         far(h, 1, 2)
-    multiply((2, 1), (1, 2), (2, 3), (3, 2))
-    for j in (1, 3):
-        for h in range(2):
-            far(h, j // 2, j)
+    multiply((2, 1), (1, 2))
+    for h in range(2):
+        far(h, 0, 1)
+    multiply((2, 3), (3, 2))
+    for h in range(2):
+        far(h, 1, 3)
     for h in range(2):
         near(h, 0, 2)
     multiply((2, 0), (0, 2), (1, 3), (3, 1))

time: 64.6 us -> 64.8 us (level)
  no operation moved by 1% of the time
where the time goes in v8:
time: 64.8 us; the launch traced here: 64.7 us
  Pallas kernels  64.1 us (99%)
    pallas_call x1, Pallas kernels, shards(): pl.pallas_call(kernel, out_shape=(jax.ShapeDtypeStruct((own, width), F32)...  63.3 us

profile of v8, /device:TPU:32, one launch (start us, length us, event | category | flops | bytes accessed | tf_op | source)
XLA Modules:
  0.0 64.7 jit_solution(1710799207574146179)
XLA Ops:
  0.6 63.3 %selected_inverse.1 = (f32[192,256]{1,0:T(8,128)S(1)}, f32[256,256]{1,0:T(8,128)S(1)}) custom-call(bf16[6,8,16,256]{3,2,1,0:T(8,128)(2,1)} %bitcast.5, s32[96,128]{1,0:T(8,128)} %bitcast.7, bf16[3072,1536]{1,0:T(8,128)(2,1)} %front.1, f32[256,256]{1,0:T(8,128)} %bitcast.6), custom_call_target="tpu_custom_call" | custom-call | tf_op jit(solution)/shard_map/selected_inverse/pallas_call | solution.py:414
  63.9 0.8 %outputs.1 = (f32[192,256]{1,0:T(8,128)}, f32[256,256]{1,0:T(8,128)}) custom-call(f32[192,256]{1,0:T(8,128)S(1)} %get-tuple-element.6.off, f32[256,256]{1,0:T(8,128)S(1)} %get-tuple-element.7.diag), custom_call_target="tpu_custom_call" | custom-call | tf_op jit(solution)/shard_map/outputs/pallas_call | solution.py:470
